TPU v7x, 128 devices: a whole 4x4x4 slice. The times are simulated.
128 devices in a mesh: region: 16 (over y, x), tile: 8 (over z, core).
Axes of the slice: x: 4, y: 4, z: 4, core: 2. Of those that a mesh axis runs over, the one named last changes fastest.
Arguments:
- state: float32 [80, 8, 32768], P(None, 'tile', 'region'), may hold values from -6 to 6
- obs_rows: float32 [16, 80, 8, 128], P('region', None, 'tile'), may hold values from -6 to 6
- obs_value: float32 [16, 8, 128], P('region', 'tile'), may hold values from -6 to 6
- obs_noise: float32 [16, 8, 128], P('region', 'tile'), may hold values from 0.3 to 3
- obs_cell: int32 [16, 8, 128], P('region', 'tile'), may hold values from 0 to 32767
- obs_class: int32 [16, 8, 128], P('region', 'tile'), may hold values from 0 to 2
- obs_count: int32 [16, 8], P('region', 'tile'), may hold values from 1 to 128, 512 in all within a row
Outputs:
- posterior: float32 [80, 8, 32768], P(None, 'tile', 'region')
Inputs may be any that keep to these rules, and one draw needn't show every extreme that they name: `obs_count`: in every batch some tile has exactly 128 live slots.
All inputs are finite; a program needn't handle non-finite values. No bound on the sum of `obs_count` on one device may be relied on, other than what follows from the above.
Results may differ from a plain program's by a relative error of at most 0.0003.
Values sent between devices are 32-bit elements; how exact they have to be, the bound alone decides.
No kernel may reach another device: no remote copies, remote signals or barrier semaphores. Data moves between devices by JAX's collectives and lax.ppermute only.
A program may use at most 64 MiB of HBM per device.

v0:
```python
import jax
import jax.numpy as jnp
from jax import lax
from jax.experimental import pallas as pl
from jax.experimental.pallas import tpu as pltpu
from jax.sharding import PartitionSpec as P

EPSILON = 1e-06
META = 8
WIDE = 256
ROOM = 32 * 1024 * 1024
F32 = jnp.float32
BF16 = jnp.bfloat16


def split(x):
    hi = x.astype(BF16).astype(F32)
    return hi, x - hi


def terms(block, members):
    rows = block[:members]
    meta = block[members : members + META]
    val, noise, pos, half, live = (meta[i : i + 1] for i in range(5))
    mean = jnp.sum(rows, axis=0, keepdims=True) / members
    an = rows - mean
    var = jnp.sum(an * an, axis=0, keepdims=True) / (members - 1) + EPSILON
    post_var = 1.0 / (1.0 / var + 1.0 / noise)
    post_mean = post_var * (mean / var + val / noise)
    shift = jnp.where(live > 0.5, post_mean - mean, 0.0)
    factor = jnp.where(live > 0.5, jnp.sqrt(post_var / var) - 1.0, 0.0)
    scale = 1.0 / ((members - 1) * var * (half * half))
    slots = rows.shape[1]
    a_hi, a_lo = split(an * scale)
    p_hi, p_rest = split(pos)
    p_mid, p_lo = split(p_rest)
    stack = jnp.concatenate(
        [
            *(a_hi, a_hi, a_lo, half, p_hi, p_mid, p_lo, pos),
            jnp.zeros((WIDE - 3 * members - 5, slots), F32),
        ],
        axis=0,
    )
    turned = jnp.transpose(stack)
    at = turned.astype(BF16)
    pb = jnp.broadcast_to(turned[:, 3 * members + 4 : 3 * members + 5], (slots, slots))
    hb = jnp.broadcast_to(turned[:, 3 * members : 3 * members + 1], (slots, slots))
    inc = shift + factor * an
    i_hi, i_lo = split(inc)
    lower = jnp.concatenate([i_lo, jnp.zeros_like(i_lo)], axis=1)
    left = jnp.concatenate([jnp.concatenate([i_hi, i_hi], axis=1), lower], axis=0).astype(BF16)
    return at, left, pb, hb


def centered(z):
    members, n = z.shape
    zc = z - jnp.sum(z, axis=0, keepdims=True) / members
    z_hi, z_lo = split(zc)
    return jnp.concatenate(
        [z_hi, z_lo, z_hi, jnp.zeros((WIDE - 3 * members, n), F32)], axis=0
    ).astype(BF16)


def change(zst, tpos, at, left, pbs, hbs):
    n = zst.shape[1]
    cov = jnp.dot(at, zst, preferred_element_type=F32)
    gains = []
    slots = pbs[0].shape[0]
    for j in range(len(pbs)):
        reps = n // pbs[j].shape[1]
        pb = jnp.concatenate([pbs[j]] * reps, axis=1) if reps > 1 else pbs[j]
        hb = jnp.concatenate([hbs[j]] * reps, axis=1) if reps > 1 else hbs[j]
        m = jnp.maximum(hb - jnp.abs(tpos - pb), 0.0)
        g = m * (m * cov[j * slots : (j + 1) * slots])
        g_hi = g.astype(BF16)
        g_lo = (g - g_hi.astype(F32)).astype(BF16)
        gains += [g_hi, g_lo]
    acc = jnp.dot(left, jnp.concatenate(gains, axis=0), preferred_element_type=F32)
    members = left.shape[0] // 2
    return acc[:members] + acc[members:]


def apply(z, tpos, *sources):
    return z + change(centered(z), tpos, *sources)


def window(refs, step, t, slots):
    at_ref, left_ref, pb_ref, hb_ref, _ = refs
    return (
        at_ref[step, t * slots : (t + 3) * slots],
        left_ref[step, :, t * 2 * slots : (t + 3) * 2 * slots],
        [pb_ref[step, t + j] for j in range(3)],
        [hb_ref[step, t + j] for j in range(3)],
    )


def vmem(shape, dtype):
    return pltpu.VMEM(shape, dtype)


def inside(*arrays):
    return [pltpu.with_memory_space_constraint(a, pltpu.VMEM) for a in arrays]


def make_crit(members, slots, last):
    full = members + META

    def crit(x_ref, y_ref, o_ref, e_ref, *rest):
        if last:
            refs = rest
        else:
            *r_refs, a, b, c, d, m, xn_ref, yn_ref, zs_ref = rest
            refs = (a, b, c, d, m)

        def keep(step, j, pack, meta):
            at, left, pb, hb = pack
            refs[0][step, j * slots : (j + 1) * slots] = at
            refs[1][step, :, j * 2 * slots : (j + 1) * 2 * slots] = left
            refs[2][step, j] = pb
            refs[3][step, j] = hb
            refs[4][step, :, j * slots : (j + 1) * slots] = meta

        first = [o_ref[1], o_ref[0], x_ref[0], x_ref[1], e_ref[0], e_ref[1]]
        packs = [terms(b, members) for b in first]
        for j in range(4):
            keep(0, j, packs[j + 1], first[j + 1][members:])
        second = [o_ref[2], x_ref[2], y_ref[...], e_ref[2]]
        for j in range(4):
            near = packs[j : j + 3]
            block = second[j]
            new = apply(
                block[:members],
                block[members + 2 : members + 3],
                jnp.concatenate([q[0] for q in near], axis=0),
                jnp.concatenate([q[1] for q in near], axis=1),
                [q[2] for q in near],
                [q[3] for q in near],
            )
            new = jnp.concatenate([new, block[members:]], axis=0)
            keep(1, j, terms(new, members), block[members:])
        if not last:
            wide = []
            for t in range(2):
                wide.append(jnp.concatenate([r_refs[t][0], r_refs[t][1]], axis=1))
                zs_ref[t] = wide[t][:members]

            def one(step, carry):
                new = [
                    apply(
                        zs_ref[t],
                        wide[t][members + 2 : members + 3],
                        *window(refs, step, t, slots),
                    )
                    for t in range(2)
                ]
                for t in range(2):
                    zs_ref[t] = new[t]
                return carry

            lax.fori_loop(0, 2, one, 0)
            for t in range(2):
                done = jnp.concatenate([zs_ref[t], wide[t][members:]], axis=0)
                xn_ref[t] = done[:, :slots]
                if t == 0:
                    xn_ref[2] = done[:, slots:]
                else:
                    yn_ref[...] = done[:, slots:]

    pack_shapes = (
        vmem((2, 4 * slots, WIDE), BF16),
        vmem((2, 2 * members, 8 * slots), BF16),
        vmem((2, 4, slots, slots), F32),
        vmem((2, 4, slots, slots), F32),
        vmem((2, META, 4 * slots), F32),
    )
    next_shapes = (vmem((3, full, slots), F32), vmem((full, slots), F32))
    return pl.pallas_call(
        crit,
        out_shape=pack_shapes if last else pack_shapes + next_shapes,
        scratch_shapes=() if last else (pltpu.VMEM((2, members, 2 * slots), F32),),
        compiler_params=pltpu.CompilerParams(vmem_limit_bytes=ROOM),
        name="crit",
    )


def run_steps(zs_ref, tpos, refs, t, slots):
    def one(step, carry):
        new = [
            apply(zs_ref[i], tpos[i], *window(refs, step, t, slots)) for i in range(len(tpos))
        ]
        for i in range(len(tpos)):
            zs_ref[i] = new[i]
        return carry

    lax.fori_loop(0, 2, one, 0)


def make_rows(members, slots, groups):
    full = members + META

    def rows(begin_ref, *all_refs):
        *refs, r_ref, n_ref, ro_ref, zs_ref = all_refs
        begin = begin_ref[0]

        def couple(c, carry):
            tpos = []
            for i in range(2):
                q = begin + 2 * c + i
                both = jnp.concatenate([ro_ref[q, 0], ro_ref[q, 1]], axis=1)
                zs_ref[i] = both[:members]
                tpos.append(both[members + 2 : members + 3])
            run_steps(zs_ref, tpos, refs, 0, slots)
            for i in range(2):
                q = begin + 2 * c + i
                for k in range(2):
                    ro_ref[q, k, :members] = zs_ref[i, :, k * slots : (k + 1) * slots]
            return carry

        lax.fori_loop(0, (groups - begin + 1) // 2, couple, 0)
        n_ref[...] = ro_ref[begin]

    smem = pl.BlockSpec(memory_space=pltpu.SMEM)
    rest = [pl.BlockSpec(memory_space=pltpu.VMEM)] * 6
    return pl.pallas_call(
        rows,
        in_specs=[smem] + rest,
        out_shape=(vmem((2, full, slots), F32), vmem((groups + 1, 2, full, slots), F32)),
        input_output_aliases={6: 1},
        scratch_shapes=(pltpu.VMEM((2, members, 2 * slots), F32),),
        compiler_params=pltpu.CompilerParams(vmem_limit_bytes=ROOM),
        name="rows",
    )


def make_cells(members, slots, cells, steps):
    part = min(cells, 2 * slots)
    chains = min(4, cells // part)
    span = 3 * slots

    def update(*all_refs):
        at_ref, left_ref, meta_ref, tri_ref, cpos_ref, s_ref, so_ref, *work = all_refs
        atc_ref, leftc_ref, pbc_ref, hbc_ref, zst_ref = work
        now_ref = s_ref if len(steps) == 1 else so_ref
        if len(steps) > 1:
            so_ref[...] = s_ref[...]

        def one_step(step):
            meta = meta_ref[step, :, :span]
            pos, half, live = meta[2:3], meta[3:4], meta[4:5]
            begin, end = cpos_ref[:, :1], cpos_ref[:, cells - 1 :]
            near = jnp.where((pos + half > begin) & (pos - half < end), live, 0.0)
            before = jnp.dot(
                jnp.broadcast_to(near, (16, span)).astype(BF16),
                tri_ref[...],
                preferred_element_type=F32,
            )
            spot = jnp.where(near > 0.5, before[:1], -1.0)
            count = (jnp.sum(near).astype(jnp.int32) + (slots - 1)) // slots
            lefts = jnp.concatenate(
                [left_ref[step, :, 2 * t * slots : (2 * t + 1) * slots] for t in range(3)], axis=1
            )

            def pick(c):
                rank = lax.broadcasted_iota(jnp.int32, (slots, span), 0) + c * slots
                hot = jnp.where(rank.astype(F32) == spot, 1.0, 0.0).astype(BF16)
                got = jnp.dot(hot, at_ref[step, :span], preferred_element_type=F32)
                atc_ref[c] = got.astype(BF16)
                k = 3 * members
                where = got[:, k + 1 : k + 2] + got[:, k + 2 : k + 3] + got[:, k + 3 : k + 4]
                pbc_ref[c] = jnp.broadcast_to(where, (slots, slots))
                hbc_ref[c] = jnp.broadcast_to(got[:, k : k + 1], (slots, slots))
                inc = lax.dot_general(
                    lefts, hot, (((1,), (1,)), ((), ())), preferred_element_type=F32
                )
                high, low = inc[:members], inc[members:]
                leftc_ref[c] = jnp.concatenate(
                    [
                        jnp.concatenate([high, high], axis=1),
                        jnp.concatenate([low, jnp.zeros_like(low)], axis=1),
                    ],
                    axis=0,
                ).astype(BF16)

            def looped(body):
                def one(c, carry):
                    body(c)
                    return carry

                lax.fori_loop(0, count, one, 0)

            looped(pick)

            def cells_step(n, carry):
                ats = [
                    pl.ds(pl.multiple_of((chains * n + i) * part, part), part) for i in range(chains)
                ]
                for i, a in enumerate(ats):
                    z = now_ref[:, a]
                    zst_ref[i] = centered(z)
                    so_ref[:, a] = z

                def add(c):
                    more = [
                        change(
                            zst_ref[i], cpos_ref[:, a], atc_ref[c], leftc_ref[c], [pbc_ref[c]], [hbc_ref[c]]
                        )
                        for i, a in enumerate(ats)
                    ]
                    for i, a in enumerate(ats):
                        so_ref[:, a] = so_ref[:, a] + more[i]

                looped(add)
                return carry

            lax.fori_loop(0, cells // (chains * part), cells_step, 0)

        if len(steps) == 1:
            one_step(steps[0])
        else:
            lax.fori_loop(0, 2, lambda step, carry: (one_step(step), carry)[1], 0)

    return pl.pallas_call(
        update,
        out_shape=vmem((members, cells), F32),
        input_output_aliases={5: 0},
        scratch_shapes=(
            pltpu.VMEM((3, slots, WIDE), BF16),
            pltpu.VMEM((3, 2 * members, 2 * slots), BF16),
            pltpu.VMEM((3, slots, slots), F32),
            pltpu.VMEM((3, slots, slots), F32),
            pltpu.VMEM((chains, WIDE, part), BF16),
        ),
        compiler_params=pltpu.CompilerParams(vmem_limit_bytes=ROOM),
        name="cells",
    )


def on_device(state, obs_rows, obs_value, obs_noise, obs_cell, obs_class, obs_count):
    members, _, cells = state.shape
    slots = obs_rows.shape[3]
    nbatch = lax.axis_size("region")
    tiles = lax.axis_size("tile")
    chips = tiles // 2
    region_index = lax.axis_index("region")
    tile_index = lax.axis_index("tile")
    tile_width = cells * nbatch
    cell_pos = (
        tile_index * tile_width + region_index * cells + jnp.arange(cells, dtype=jnp.int32)
    ).astype(F32)[None]
    pos = (tile_index * tile_width + obs_cell[0, 0]).astype(F32)
    half = (tile_width / 4) * (obs_class[0, 0] + 2).astype(F32)
    live = (jnp.arange(slots, dtype=jnp.int32) < obs_count[0, 0]).astype(F32)
    zero = jnp.zeros_like(pos)
    block = jnp.concatenate(
        [
            obs_rows[0, :, 0, :],
            jnp.stack([obs_value[0, 0], obs_noise[0, 0], pos, half, live, zero, zero, zero]),
        ],
        axis=0,
    )
    own = lax.all_to_all(
        jnp.broadcast_to(block[None], (nbatch,) + block.shape), "region", 0, 0, tiled=True
    )
    partner = [(i, i ^ 1) for i in range(tiles)]
    across = []
    for z in range(chips):
        across += [(2 * z + 1, 2 * ((z + 1) % chips)), (2 * z, 2 * ((z - 1) % chips) + 1)]
    groups = nbatch // 2
    begun = min(nbatch, 4)
    other = lax.ppermute(own[:begun], "tile", partner)
    x = jnp.stack([own[0], other[0], own[1]])
    y = other[1]
    near = own[2:4]
    far = other[2:4]
    rest = jnp.concatenate([own, jnp.zeros_like(own[:2])]).reshape(groups + 1, 2, *block.shape)
    cells_now = state[:, 0, :]
    order = jnp.arange(3 * slots, dtype=jnp.int32)
    tri = (order[:, None] < order[None, :]).astype(BF16)

    def update(steps, packs, cells_now):
        at, left, _, _, meta = packs
        kernel = make_cells(members, slots, cells, steps)
        return kernel(*inside(at, left, meta, tri, cell_pos, cells_now))

    crit = make_crit(members, slots, False)
    rows = make_rows(members, slots, groups)

    def middle(g, carry):
        x, y, rest, cells_now, *packs = carry
        o = lax.ppermute(x, "tile", across)
        if g > 2:
            cells_now = update((0,), packs, cells_now)
            o, cells_now = lax.optimization_barrier((o, cells_now))
        near, rest = rows(jnp.full((1,), g + 1, jnp.int32), *inside(*packs, rest))
        o, near = lax.optimization_barrier((o, near))
        far = lax.ppermute(near, "tile", partner)
        e = lax.ppermute(o, "tile", partner)
        cells_now = update((1,) if g > 2 else (0, 1), packs, cells_now)
        e, far, cells_now = lax.optimization_barrier((e, far, cells_now))
        *packs, x, y = crit(*inside(x, y, o, e, near, far))
        return (x, y, rest, cells_now, *packs)

    o = lax.ppermute(x, "tile", across)
    e = lax.ppermute(o, "tile", partner)
    *packs, x, y = crit(*inside(x, y, o, e, near, far))
    carry = (x, y, rest, cells_now, *packs)
    for g in range(1, groups - 1):
        carry = middle(g, carry)
    x, y, rest, cells_now, *packs = carry
    o = lax.ppermute(x, "tile", across)
    cells_now = update((0,), packs, cells_now)
    o, cells_now = lax.optimization_barrier((o, cells_now))
    e = lax.ppermute(o, "tile", partner)
    cells_now = update((1,), packs, cells_now)
    e, cells_now = lax.optimization_barrier((e, cells_now))
    packs = make_crit(members, slots, True)(*inside(x, y, o, e))
    cells_now = update((0, 1), packs, cells_now)
    return cells_now[:, None, :]


def solution(mesh):
    placed = (
        P(None, "tile", "region"),
        P("region", None, "tile", None),
        P("region", "tile", None),
        P("region", "tile", None),
        P("region", "tile", None),
        P("region", "tile", None),
        P("region", "tile"),
    )
    return jax.shard_map(
        on_device, mesh=mesh, in_specs=placed, out_specs=P(None, "tile", "region"), check_vma=False
    )
```

profile of v0, /device:TPU:1, one launch (start us, length us, event | category | flops | bytes accessed | tf_op | source)
XLA Modules:
  0.0 129.7 jit_solution(10456806049927871789)
XLA Ops:
  1.3 0.7 copy-done.4
  2.0 0.6 copy-done.1
  2.6 0.8 concatenate.10
  3.5 20.2 %all_to_all.5 = f32[16,88,128]{2,1,0:T(8,128)S(1)} all-to-all(f32[16,88,128]{2,1,0:T(8,128)S(1)} %broadcast_in_dim.4), channel_id=1, replica_groups=mesh['region'=16,'tile'=8] {'region'}, dimensions={0} | all-to-all | bytes 1441792 | tf_op jit(solution)/shard_map/all_to_all | solution.py:361
  23.7 1.9 %collective-permute-start = (f32[4,88,128]{2,1,0:T(8,128)S(1)}, f32[4,88,128]{2,1,0:T(8,128)S(1)}, u32[]{:S(2)}, u32[]{:S(2)}) collective-permute-start(f32[4,88,128]{2,1,0:T(8,128)S(1)} %slice.29), channel_id=1, source_target_pairs={{0,1},{1,0},{2,3},{3,2},{4,5},{5,4},{6,7},{7,6},{8,9},{9,8},{10,11... | collective-permute-start | bytes 540680 | tf_op jit(solution)/shard_map/ppermute | solution.py:370
  25.6 1.0 collective-permute-done
  26.6 2.0 %collective-permute-start.1 = (f32[3,88,128]{2,1,0:T(8,128)S(1)}, f32[3,88,128]{2,1,0:T(8,128)S(1)}, u32[]{:S(2)}, u32[]{:S(2)}) collective-permute-start(f32[3,88,128]{2,1,0:T(8,128)S(1)} %pad_maximum_fusion.x_ref), channel_id=1, source_target_pairs={{1,2},{0,7},{3,4},{2,1},{5,6},{4,3},{7,0},{6,5},{9,10},{8,15},{11,... | collective-permute-start | bytes 405512 | tf_op jit(solution)/shard_map/ppermute | solution.py:403
  28.6 2.7 %collective-permute-done.1.o_ref = f32[3,88,128]{2,1,0:T(8,128)S(1)} collective-permute-done((f32[3,88,128]{2,1,0:T(8,128)S(1)}, f32[3,88,128]{2,1,0:T(8,128)S(1)}, u32[]{:S(2)}, u32[]{:S(2)}) %collective-permute-start.1) | collective-permute-done | bytes 135200 | tf_op jit(solution)/shard_map/ppermute | solution.py:403
  31.3 2.3 %collective-permute-start.2 = (f32[3,88,128]{2,1,0:T(8,128)S(1)}, f32[3,88,128]{2,1,0:T(8,128)S(1)}, u32[]{:S(2)}, u32[]{:S(2)}) collective-permute-start(f32[3,88,128]{2,1,0:T(8,128)S(1)} %collective-permute-done.1.o_ref), channel_id=1, source_target_pairs={{0,1},{1,0},{2,3},{3,2},{4,5},{5,4},{6,7},{7,6},{8,9},{9,8},{10,11... | collective-permute-start | bytes 405512 | tf_op jit(solution)/shard_map/ppermute | solution.py:404
  33.6 1.0 collective-permute-done.2.e_ref
  34.6 2.6 %crit.8 = (bf16[2,512,256]{2,1,0:T(8,128)(2,1)S(1)}, bf16[2,160,1024]{2,1,0:T(8,128)(2,1)S(1)}, f32[2,4,128,128]{3,2,1,0:T(8,128)S(1)}, f32[2,4,128,128]{3,2,1,0...) custom-call(f32[3,88,128]{2,1,0:T(8,128)S(1)} %pad_maximum_fusion.x_ref, ...), custom_call_target="tpu_custom_call" | custom-call | tf_op jit(solution)/shard_map/crit/pallas_call | solution.py:405
  37.4 3.5 %rows.6 = (f32[2,88,128]{2,1,0:T(8,128)S(1)}, f32[9,2,88,128]{3,2,1,0:T(8,128)S(1)}) custom-call(s32[1]{0:T(128)} %constant.6.clone.1.begin_ref, bf16[2,512,256]{2,1,0:T(8,128)(2,1)S(1)} %get-tuple-element.110.all_refs_0_, bf16[2,160,1024]{2,1,0:T(8,128)(2,1)S(1)} %get-tuple-element.111.all_refs_1_, ...), custom_call_target="tpu_custom_call", output_to_operand_aliasing={{1}: (6, {})} | custom-call | tf_op jit(solution)/shard_map/rows/pallas_call | solution.py:394
  40.9 1.1 collective-permute-done.3.o_ref
  42.0 2.3 %collective-permute-start.4 = (f32[3,88,128]{2,1,0:T(8,128)S(1)}, f32[3,88,128]{2,1,0:T(8,128)S(1)}, u32[]{:S(2)}, u32[]{:S(2)}) collective-permute-start(f32[3,88,128]{2,1,0:T(8,128)S(1)} %collective-permute-done.3.o_ref), channel_id=1, source_target_pairs={{0,1},{1,0},{2,3},{3,2},{4,5},{5,4},{6,7},{7,6},{8,9},{9,8},{10,11... | collective-permute-start | bytes 405512 | tf_op jit(solution)/shard_map/ppermute | solution.py:397
  44.7 3.5 %cells.13.all_refs_5_ = f32[80,2048]{1,0:T(8,128)S(1)} custom-call(bf16[2,512,256]{2,1,0:T(8,128)(2,1)S(1)} %get-tuple-element.110.all_refs_0_, bf16[2,160,1024]{2,1,0:T(8,128)(2,1)S(1)} %get-tuple-element.111.all_refs_1_, f32[2,8,512]{2,1,0:T(8,128)S(1)} %get-tuple-element.114.all_refs_4_.all_refs_2_, ...), custom_call_target="tpu_custom_call", output_to_operand_aliasing={{}: (5, {})} | custom-call | tf_op jit(solution)/shard_map/cells/pallas_call | solution.py:383
  48.2 2.7 %crit.9 = (bf16[2,512,256]{2,1,0:T(8,128)(2,1)S(1)}, bf16[2,160,1024]{2,1,0:T(8,128)(2,1)S(1)}, f32[2,4,128,128]{3,2,1,0:T(8,128)S(1)}, f32[2,4,128,128]{3,2,1,0...) custom-call(f32[3,88,128]{2,1,0:T(8,128)S(1)} %get-tuple-element.108.x_ref, ...), custom_call_target="tpu_custom_call" | custom-call | tf_op jit(solution)/shard_map/crit/pallas_call | solution.py:400
  51.0 3.6 %rows.7 = (f32[2,88,128]{2,1,0:T(8,128)S(1)}, f32[9,2,88,128]{3,2,1,0:T(8,128)S(1)}) custom-call(s32[1]{0:T(128)} %constant.10.clone.1.begin_ref, bf16[2,512,256]{2,1,0:T(8,128)(2,1)S(1)} %get-tuple-element.122.all_refs_0_, bf16[2,160,1024]{2,1,0:T(8,128)(2,1)S(1)} %get-tuple-element.123.all_refs_1_, ...), custom_call_target="tpu_custom_call", output_to_operand_aliasing={{1}: (6, {})} | custom-call | tf_op jit(solution)/shard_map/rows/pallas_call | solution.py:394
  54.7 1.1 collective-permute-done.6.o_ref
  55.7 1.4 %collective-permute-start.7 = (f32[3,88,128]{2,1,0:T(8,128)S(1)}, f32[3,88,128]{2,1,0:T(8,128)S(1)}, u32[]{:S(2)}, u32[]{:S(2)}) collective-permute-start(f32[3,88,128]{2,1,0:T(8,128)S(1)} %collective-permute-done.6.o_ref), channel_id=1, source_target_pairs={{0,1},{1,0},{2,3},{3,2},{4,5},{5,4},{6,7},{7,6},{8,9},{9,8},{10,11... | collective-permute-start | bytes 405512 | tf_op jit(solution)/shard_map/ppermute | solution.py:397
  57.3 3.5 %cells.14.all_refs_5_ = f32[80,2048]{1,0:T(8,128)S(1)} custom-call(bf16[2,512,256]{2,1,0:T(8,128)(2,1)S(1)} %get-tuple-element.122.all_refs_0_, bf16[2,160,1024]{2,1,0:T(8,128)(2,1)S(1)} %get-tuple-element.123.all_refs_1_, f32[2,8,512]{2,1,0:T(8,128)S(1)} %get-tuple-element.126.all_refs_4_.all_refs_2_, ...), custom_call_target="tpu_custom_call", output_to_operand_aliasing={{}: (5, {})} | custom-call | tf_op jit(solution)/shard_map/cells/pallas_call | solution.py:383
  60.8 2.7 %crit.10 = (bf16[2,512,256]{2,1,0:T(8,128)(2,1)S(1)}, bf16[2,160,1024]{2,1,0:T(8,128)(2,1)S(1)}, f32[2,4,128,128]{3,2,1,0:T(8,128)S(1)}, f32[2,4,128,128]{3,2,1,...) custom-call(f32[3,88,128]{2,1,0:T(8,128)S(1)} %get-tuple-element.120.x_ref, ...), custom_call_target="tpu_custom_call" | custom-call | tf_op jit(solution)/shard_map/crit/pallas_call | solution.py:400
  63.8 1.9 %cells.15.all_refs_5_ = f32[80,2048]{1,0:T(8,128)S(1)} custom-call(bf16[2,512,256]{2,1,0:T(8,128)(2,1)S(1)} %get-tuple-element.136.all_refs_0_, bf16[2,160,1024]{2,1,0:T(8,128)(2,1)S(1)} %get-tuple-element.137.all_refs_1_, f32[2,8,512]{2,1,0:T(8,128)S(1)} %get-tuple-element.138.all_refs_2_.all_refs_4_, ...), custom_call_target="tpu_custom_call", output_to_operand_aliasing={{}: (5, {})} | custom-call | tf_op jit(solution)/shard_map/cells/pallas_call | solution.py:383
  65.7 2.4 %rows.8 = (f32[2,88,128]{2,1,0:T(8,128)S(1)}, f32[9,2,88,128]{3,2,1,0:T(8,128)S(1)}) custom-call(s32[1]{0:T(128)} %constant.11.clone.1.begin_ref, bf16[2,512,256]{2,1,0:T(8,128)(2,1)S(1)} %get-tuple-element.136.all_refs_0_, bf16[2,160,1024]{2,1,0:T(8,128)(2,1)S(1)} %get-tuple-element.137.all_refs_1_, ...), custom_call_target="tpu_custom_call", output_to_operand_aliasing={{1}: (6, {})} | custom-call | tf_op jit(solution)/shard_map/rows/pallas_call | solution.py:394
  68.3 3.4 %collective-permute-start.10 = (f32[3,88,128]{2,1,0:T(8,128)S(1)}, f32[3,88,128]{2,1,0:T(8,128)S(1)}, u32[]{:S(2)}, u32[]{:S(2)}) collective-permute-start(f32[3,88,128]{2,1,0:T(8,128)S(1)} %collective-permute-done.9.o_ref), channel_id=1, source_target_pairs={{0,1},{1,0},{2,3},{3,2},{4,5},{5,4},{6,7},{7,6},{8,9},{9,8},{10,11... | collective-permute-start | bytes 405512 | tf_op jit(solution)/shard_map/ppermute | solution.py:397
  71.8 3.1 %cells.16.all_refs_5_ = f32[80,2048]{1,0:T(8,128)S(1)} custom-call(bf16[2,512,256]{2,1,0:T(8,128)(2,1)S(1)} %get-tuple-element.136.all_refs_0_, bf16[2,160,1024]{2,1,0:T(8,128)(2,1)S(1)} %get-tuple-element.137.all_refs_1_, f32[2,8,512]{2,1,0:T(8,128)S(1)} %get-tuple-element.138.all_refs_2_.all_refs_4_, ...), custom_call_target="tpu_custom_call", output_to_operand_aliasing={{}: (5, {})} | custom-call | tf_op jit(solution)/shard_map/cells/pallas_call | solution.py:383
  75.0 2.7 %crit.11 = (bf16[2,512,256]{2,1,0:T(8,128)(2,1)S(1)}, bf16[2,160,1024]{2,1,0:T(8,128)(2,1)S(1)}, f32[2,4,128,128]{3,2,1,0:T(8,128)S(1)}, f32[2,4,128,128]{3,2,1,...) custom-call(f32[3,88,128]{2,1,0:T(8,128)S(1)} %get-tuple-element.134.x_ref, ...), custom_call_target="tpu_custom_call" | custom-call | tf_op jit(solution)/shard_map/crit/pallas_call | solution.py:400
  77.9 1.8 %cells.17.all_refs_5_ = f32[80,2048]{1,0:T(8,128)S(1)} custom-call(bf16[2,512,256]{2,1,0:T(8,128)(2,1)S(1)} %get-tuple-element.152.all_refs_0_, bf16[2,160,1024]{2,1,0:T(8,128)(2,1)S(1)} %get-tuple-element.153.all_refs_1_, f32[2,8,512]{2,1,0:T(8,128)S(1)} %get-tuple-element.154.all_refs_2_.all_refs_4_, ...), custom_call_target="tpu_custom_call", output_to_operand_aliasing={{}: (5, {})} | custom-call | tf_op jit(solution)/shard_map/cells/pallas_call | solution.py:383
  79.6 2.4 %rows.9 = (f32[2,88,128]{2,1,0:T(8,128)S(1)}, f32[9,2,88,128]{3,2,1,0:T(8,128)S(1)}) custom-call(s32[1]{0:T(128)} %constant.12.clone.1.begin_ref, bf16[2,512,256]{2,1,0:T(8,128)(2,1)S(1)} %get-tuple-element.152.all_refs_0_, bf16[2,160,1024]{2,1,0:T(8,128)(2,1)S(1)} %get-tuple-element.153.all_refs_1_, ...), custom_call_target="tpu_custom_call", output_to_operand_aliasing={{1}: (6, {})} | custom-call | tf_op jit(solution)/shard_map/rows/pallas_call | solution.py:394
  82.7 1.8 %cells.18.all_refs_5_ = f32[80,2048]{1,0:T(8,128)S(1)} custom-call(bf16[2,512,256]{2,1,0:T(8,128)(2,1)S(1)} %get-tuple-element.152.all_refs_0_, bf16[2,160,1024]{2,1,0:T(8,128)(2,1)S(1)} %get-tuple-element.153.all_refs_1_, f32[2,8,512]{2,1,0:T(8,128)S(1)} %get-tuple-element.154.all_refs_2_.all_refs_4_, ...), custom_call_target="tpu_custom_call", output_to_operand_aliasing={{}: (5, {})} | custom-call | tf_op jit(solution)/shard_map/cells/pallas_call | solution.py:383
  84.5 2.7 %crit.12 = (bf16[2,512,256]{2,1,0:T(8,128)(2,1)S(1)}, bf16[2,160,1024]{2,1,0:T(8,128)(2,1)S(1)}, f32[2,4,128,128]{3,2,1,0:T(8,128)S(1)}, f32[2,4,128,128]{3,2,1,...) custom-call(f32[3,88,128]{2,1,0:T(8,128)S(1)} %get-tuple-element.150.x_ref, ...), custom_call_target="tpu_custom_call" | custom-call | tf_op jit(solution)/shard_map/crit/pallas_call | solution.py:400
  87.2 1.7 %collective-permute-start.15 = (f32[3,88,128]{2,1,0:T(8,128)S(1)}, f32[3,88,128]{2,1,0:T(8,128)S(1)}, u32[]{:S(2)}, u32[]{:S(2)}) collective-permute-start(f32[3,88,128]{2,1,0:T(8,128)S(1)} %get-tuple-element.166.x_ref), channel_id=1, source_target_pairs={{1,2},{0,7},{3,4},{2,1},{5,6},{4,3},{7,0},{6,5},{9,10},{8,15},{11,... | collective-permute-start | bytes 405512 | tf_op jit(solution)/shard_map/ppermute | solution.py:390
  88.9 1.8 %cells.19.all_refs_5_ = f32[80,2048]{1,0:T(8,128)S(1)} custom-call(bf16[2,512,256]{2,1,0:T(8,128)(2,1)S(1)} %get-tuple-element.168.all_refs_0_, bf16[2,160,1024]{2,1,0:T(8,128)(2,1)S(1)} %get-tuple-element.169.all_refs_1_, f32[2,8,512]{2,1,0:T(8,128)S(1)} %get-tuple-element.170.all_refs_2_.all_refs_4_, ...), custom_call_target="tpu_custom_call", output_to_operand_aliasing={{}: (5, {})} | custom-call | tf_op jit(solution)/shard_map/cells/pallas_call | solution.py:383
  90.6 1.2 rows.10
  92.0 1.6 %collective-permute-start.16 = (f32[3,88,128]{2,1,0:T(8,128)S(1)}, f32[3,88,128]{2,1,0:T(8,128)S(1)}, u32[]{:S(2)}, u32[]{:S(2)}) collective-permute-start(f32[3,88,128]{2,1,0:T(8,128)S(1)} %collective-permute-done.15.o_ref), channel_id=1, source_target_pairs={{0,1},{1,0},{2,3},{3,2},{4,5},{5,4},{6,7},{7,6},{8,9},{9,8},{10,11... | collective-permute-start | bytes 405512 | tf_op jit(solution)/shard_map/ppermute | solution.py:397
  93.7 3.3 %cells.20.all_refs_5_ = f32[80,2048]{1,0:T(8,128)S(1)} custom-call(bf16[2,512,256]{2,1,0:T(8,128)(2,1)S(1)} %get-tuple-element.168.all_refs_0_, bf16[2,160,1024]{2,1,0:T(8,128)(2,1)S(1)} %get-tuple-element.169.all_refs_1_, f32[2,8,512]{2,1,0:T(8,128)S(1)} %get-tuple-element.170.all_refs_2_.all_refs_4_, ...), custom_call_target="tpu_custom_call", output_to_operand_aliasing={{}: (5, {})} | custom-call | tf_op jit(solution)/shard_map/cells/pallas_call | solution.py:383
  97.0 2.7 %crit.13 = (bf16[2,512,256]{2,1,0:T(8,128)(2,1)S(1)}, bf16[2,160,1024]{2,1,0:T(8,128)(2,1)S(1)}, f32[2,4,128,128]{3,2,1,0:T(8,128)S(1)}, f32[2,4,128,128]{3,2,1,...) custom-call(f32[3,88,128]{2,1,0:T(8,128)S(1)} %get-tuple-element.166.x_ref, ...), custom_call_target="tpu_custom_call" | custom-call | tf_op jit(solution)/shard_map/crit/pallas_call | solution.py:400
  100.3 3.1 %cells.21.all_refs_5_ = f32[80,2048]{1,0:T(8,128)S(1)} custom-call(bf16[2,512,256]{2,1,0:T(8,128)(2,1)S(1)} %get-tuple-element.184.all_refs_0_, bf16[2,160,1024]{2,1,0:T(8,128)(2,1)S(1)} %get-tuple-element.185.all_refs_1_, f32[2,8,512]{2,1,0:T(8,128)S(1)} %get-tuple-element.186.all_refs_2_.all_refs_4_, ...), custom_call_target="tpu_custom_call", output_to_operand_aliasing={{}: (5, {})} | custom-call | tf_op jit(solution)/shard_map/cells/pallas_call | solution.py:383
  103.4 1.2 rows.11
  104.7 1.2 collective-permute-start.19
  106.0 1.8 %cells.22.all_refs_5_ = f32[80,2048]{1,0:T(8,128)S(1)} custom-call(bf16[2,512,256]{2,1,0:T(8,128)(2,1)S(1)} %get-tuple-element.184.all_refs_0_, bf16[2,160,1024]{2,1,0:T(8,128)(2,1)S(1)} %get-tuple-element.185.all_refs_1_, f32[2,8,512]{2,1,0:T(8,128)S(1)} %get-tuple-element.186.all_refs_2_.all_refs_4_, ...), custom_call_target="tpu_custom_call", output_to_operand_aliasing={{}: (5, {})} | custom-call | tf_op jit(solution)/shard_map/cells/pallas_call | solution.py:383
  107.8 3.1 %crit.14 = (bf16[2,512,256]{2,1,0:T(8,128)(2,1)S(1)}, bf16[2,160,1024]{2,1,0:T(8,128)(2,1)S(1)}, f32[2,4,128,128]{3,2,1,0:T(8,128)}, f32[2,4,128,128]{3,2,1,0:T(...) custom-call(f32[3,88,128]{2,1,0:T(8,128)S(1)} %get-tuple-element.182.x_ref, ...), custom_call_target="tpu_custom_call" | custom-call | tf_op jit(solution)/shard_map/crit/pallas_call | solution.py:400
  111.4 3.1 %cells.23.all_refs_5_ = f32[80,2048]{1,0:T(8,128)S(1)} custom-call(bf16[2,512,256]{2,1,0:T(8,128)(2,1)S(1)} %get-tuple-element.200.all_refs_0_, bf16[2,160,1024]{2,1,0:T(8,128)(2,1)S(1)} %get-tuple-element.201.all_refs_1_, f32[2,8,512]{2,1,0:T(8,128)S(1)} %get-tuple-element.202.all_refs_2_, ...), custom_call_target="tpu_custom_call", output_to_operand_aliasing={{}: (5, {})} | custom-call | tf_op jit(solution)/shard_map/cells/pallas_call | solution.py:383
  114.5 0.7 collective-permute-done.21.o_ref
  115.2 2.5 %collective-permute-start.22 = (f32[3,88,128]{2,1,0:T(8,128)S(1)}, f32[3,88,128]{2,1,0:T(8,128)S(1)}, u32[]{:S(2)}, u32[]{:S(2)}) collective-permute-start(f32[3,88,128]{2,1,0:T(8,128)S(1)} %collective-permute-done.21.o_ref), channel_id=1, source_target_pairs={{0,1},{1,0},{2,3},{3,2},{4,5},{5,4},{6,7},{7,6},{8,9},{9,8},{10,11... | collective-permute-start | bytes 405512 | tf_op jit(solution)/shard_map/ppermute | solution.py:413
  117.8 1.8 %cells.24.all_refs_5_ = f32[80,2048]{1,0:T(8,128)S(1)} custom-call(bf16[2,512,256]{2,1,0:T(8,128)(2,1)S(1)} %get-tuple-element.200.all_refs_0_, bf16[2,160,1024]{2,1,0:T(8,128)(2,1)S(1)} %get-tuple-element.201.all_refs_1_, f32[2,8,512]{2,1,0:T(8,128)S(1)} %get-tuple-element.202.all_refs_2_, ...), custom_call_target="tpu_custom_call", output_to_operand_aliasing={{}: (5, {})} | custom-call | tf_op jit(solution)/shard_map/cells/pallas_call | solution.py:383
  119.6 2.4 %crit.15 = (bf16[2,512,256]{2,1,0:T(8,128)(2,1)S(1)}, bf16[2,160,1024]{2,1,0:T(8,128)(2,1)S(1)}, f32[2,4,128,128]{3,2,1,0:T(8,128)}, f32[2,4,128,128]{3,2,1,0:T(8,128)}, f32[2,8,512]{2,1,0:T(8,128)S(1)}) custom-call(f32[3,88,128]{2,1,0:T(8,128)S(1)} %get-tuple-element.198.x_ref, f32[88,128]{1,0:T(8,128)S(1)} %get-tuple-element.199.y_ref, ...), custom_call_target="tpu_custom_call" | custom-call | tf_op jit(solution)/shard_map/crit/pallas_call | solution.py:416
  122.0 6.2 %cells.25 = f32[80,2048]{1,0:T(8,128)S(1)} custom-call(bf16[2,512,256]{2,1,0:T(8,128)(2,1)S(1)} %get-tuple-element.207.all_refs_0_, bf16[2,160,1024]{2,1,0:T(8,128)(2,1)S(1)} %get-tuple-element.208.all_refs_1_, f32[2,8,512]{2,1,0:T(8,128)S(1)} %get-tuple-element.209.all_refs_2_, ...), custom_call_target="tpu_custom_call", output_to_operand_aliasing={{}: (5, {})} | custom-call | tf_op jit(solution)/shard_map/cells/pallas_call | solution.py:383
  128.2 1.5 %copy.27 = f32[80,1,2048]{2,1,0:T(1,128)} copy(f32[80,1,2048]{2,0,1:T(8,128)S(1)} %bitcast.17) | data formatting | bytes 1310720 | tf_op jit(solution)/shard_map/broadcast_in_dim | solution.py:418
  (54 shorter events, 4.4 us)
Async XLA Ops:
  0.7 0.7 copy-start.3
  1.3 0.7 copy-start.4
  2.0 0.7 copy-start.1
  2.0 0.7 copy-start.2
  23.7 2.9 %collective-permute-start = (f32[4,88,128]{2,1,0:T(8,128)S(1)}, f32[4,88,128]{2,1,0:T(8,128)S(1)}, u32[]{:S(2)}, u32[]{:S(2)}) collective-permute-start(f32[4,88,128]{2,1,0:T(8,128)S(1)} %slice.29), channel_id=1, source_target_pairs={{0,1},{1,0},{2,3},{3,2},{4,5},{5,4},{6,7},{7,6},{8,9},{9,8},{10,11... | collective-permute-start | bytes 540680 | tf_op jit(solution)/shard_map/ppermute | solution.py:370
  26.6 4.7 %collective-permute-start.1 = (f32[3,88,128]{2,1,0:T(8,128)S(1)}, f32[3,88,128]{2,1,0:T(8,128)S(1)}, u32[]{:S(2)}, u32[]{:S(2)}) collective-permute-start(f32[3,88,128]{2,1,0:T(8,128)S(1)} %pad_maximum_fusion.x_ref), channel_id=1, source_target_pairs={{1,2},{0,7},{3,4},{2,1},{5,6},{4,3},{7,0},{6,5},{9,10},{8,15},{11,... | collective-permute-start | bytes 405512 | tf_op jit(solution)/shard_map/ppermute | solution.py:403
  31.3 3.3 %collective-permute-start.2 = (f32[3,88,128]{2,1,0:T(8,128)S(1)}, f32[3,88,128]{2,1,0:T(8,128)S(1)}, u32[]{:S(2)}, u32[]{:S(2)}) collective-permute-start(f32[3,88,128]{2,1,0:T(8,128)S(1)} %collective-permute-done.1.o_ref), channel_id=1, source_target_pairs={{0,1},{1,0},{2,3},{3,2},{4,5},{5,4},{6,7},{7,6},{8,9},{9,8},{10,11... | collective-permute-start | bytes 405512 | tf_op jit(solution)/shard_map/ppermute | solution.py:404
  37.2 4.8 %collective-permute-start.3 = (f32[3,88,128]{2,1,0:T(8,128)S(1)}, f32[3,88,128]{2,1,0:T(8,128)S(1)}, u32[]{:S(2)}, u32[]{:S(2)}) collective-permute-start(f32[3,88,128]{2,1,0:T(8,128)S(1)} %get-tuple-element.108.x_ref), channel_id=1, source_target_pairs={{1,2},{0,7},{3,4},{2,1},{5,6},{4,3},{7,0},{6,5},{9,10},{8,15},{11,... | collective-permute-start | bytes 405512 | tf_op jit(solution)/shard_map/ppermute | solution.py:390
  37.4 6.9 %copy-start = (f32[80,1,2048]{2,1,0:T(1,128)S(1)}, f32[80,1,2048]{2,1,0:T(1,128)}, u32[]{:S(2)}) copy-start(f32[80,1,2048]{2,1,0:T(1,128)} %param.7) | copy-start | bytes 1966084
  42.0 6.2 %collective-permute-start.4 = (f32[3,88,128]{2,1,0:T(8,128)S(1)}, f32[3,88,128]{2,1,0:T(8,128)S(1)}, u32[]{:S(2)}, u32[]{:S(2)}) collective-permute-start(f32[3,88,128]{2,1,0:T(8,128)S(1)} %collective-permute-done.3.o_ref), channel_id=1, source_target_pairs={{0,1},{1,0},{2,3},{3,2},{4,5},{5,4},{6,7},{7,6},{8,9},{9,8},{10,11... | collective-permute-start | bytes 405512 | tf_op jit(solution)/shard_map/ppermute | solution.py:397
  44.5 3.7 %collective-permute-start.5 = (f32[2,88,128]{2,1,0:T(8,128)S(1)}, f32[2,88,128]{2,1,0:T(8,128)S(1)}, u32[]{:S(2)}, u32[]{:S(2)}) collective-permute-start(f32[2,88,128]{2,1,0:T(8,128)S(1)} %get-tuple-element.117.rest_0_), channel_id=1, source_target_pairs={{0,1},{1,0},{2,3},{3,2},{4,5},{5,4},{6,7},{7,6},{8,9},{9,8},{10,11... | collective-permute-start | bytes 270344 | tf_op jit(solution)/shard_map/ppermute | solution.py:396
  50.9 4.8 %collective-permute-start.6 = (f32[3,88,128]{2,1,0:T(8,128)S(1)}, f32[3,88,128]{2,1,0:T(8,128)S(1)}, u32[]{:S(2)}, u32[]{:S(2)}) collective-permute-start(f32[3,88,128]{2,1,0:T(8,128)S(1)} %get-tuple-element.120.x_ref), channel_id=1, source_target_pairs={{1,2},{0,7},{3,4},{2,1},{5,6},{4,3},{7,0},{6,5},{9,10},{8,15},{11,... | collective-permute-start | bytes 405512 | tf_op jit(solution)/shard_map/ppermute | solution.py:390
  55.7 5.1 %collective-permute-start.7 = (f32[3,88,128]{2,1,0:T(8,128)S(1)}, f32[3,88,128]{2,1,0:T(8,128)S(1)}, u32[]{:S(2)}, u32[]{:S(2)}) collective-permute-start(f32[3,88,128]{2,1,0:T(8,128)S(1)} %collective-permute-done.6.o_ref), channel_id=1, source_target_pairs={{0,1},{1,0},{2,3},{3,2},{4,5},{5,4},{6,7},{7,6},{8,9},{9,8},{10,11... | collective-permute-start | bytes 405512 | tf_op jit(solution)/shard_map/ppermute | solution.py:397
  57.2 3.6 %collective-permute-start.8 = (f32[2,88,128]{2,1,0:T(8,128)S(1)}, f32[2,88,128]{2,1,0:T(8,128)S(1)}, u32[]{:S(2)}, u32[]{:S(2)}) collective-permute-start(f32[2,88,128]{2,1,0:T(8,128)S(1)} %get-tuple-element.130.rest_0_), channel_id=1, source_target_pairs={{0,1},{1,0},{2,3},{3,2},{4,5},{5,4},{6,7},{7,6},{8,9},{9,8},{10,11... | collective-permute-start | bytes 270344 | tf_op jit(solution)/shard_map/ppermute | solution.py:396
  63.5 4.8 %collective-permute-start.9 = (f32[3,88,128]{2,1,0:T(8,128)S(1)}, f32[3,88,128]{2,1,0:T(8,128)S(1)}, u32[]{:S(2)}, u32[]{:S(2)}) collective-permute-start(f32[3,88,128]{2,1,0:T(8,128)S(1)} %get-tuple-element.134.x_ref), channel_id=1, source_target_pairs={{1,2},{0,7},{3,4},{2,1},{5,6},{4,3},{7,0},{6,5},{9,10},{8,15},{11,... | collective-permute-start | bytes 405512 | tf_op jit(solution)/shard_map/ppermute | solution.py:390
  68.3 6.6 %collective-permute-start.10 = (f32[3,88,128]{2,1,0:T(8,128)S(1)}, f32[3,88,128]{2,1,0:T(8,128)S(1)}, u32[]{:S(2)}, u32[]{:S(2)}) collective-permute-start(f32[3,88,128]{2,1,0:T(8,128)S(1)} %collective-permute-done.9.o_ref), channel_id=1, source_target_pairs={{0,1},{1,0},{2,3},{3,2},{4,5},{5,4},{6,7},{7,6},{8,9},{9,8},{10,11... | collective-permute-start | bytes 405512 | tf_op jit(solution)/shard_map/ppermute | solution.py:397
  71.7 3.2 %collective-permute-start.11 = (f32[2,88,128]{2,1,0:T(8,128)S(1)}, f32[2,88,128]{2,1,0:T(8,128)S(1)}, u32[]{:S(2)}, u32[]{:S(2)}) collective-permute-start(f32[2,88,128]{2,1,0:T(8,128)S(1)} %get-tuple-element.146.rest_0_), channel_id=1, source_target_pairs={{0,1},{1,0},{2,3},{3,2},{4,5},{5,4},{6,7},{7,6},{8,9},{9,8},{10,11... | collective-permute-start | bytes 270344 | tf_op jit(solution)/shard_map/ppermute | solution.py:396
  77.7 4.5 %collective-permute-start.12 = (f32[3,88,128]{2,1,0:T(8,128)S(1)}, f32[3,88,128]{2,1,0:T(8,128)S(1)}, u32[]{:S(2)}, u32[]{:S(2)}) collective-permute-start(f32[3,88,128]{2,1,0:T(8,128)S(1)} %get-tuple-element.150.x_ref), channel_id=1, source_target_pairs={{1,2},{0,7},{3,4},{2,1},{5,6},{4,3},{7,0},{6,5},{9,10},{8,15},{11,... | collective-permute-start | bytes 405512 | tf_op jit(solution)/shard_map/ppermute | solution.py:390
  82.2 2.3 %collective-permute-start.13 = (f32[3,88,128]{2,1,0:T(8,128)S(1)}, f32[3,88,128]{2,1,0:T(8,128)S(1)}, u32[]{:S(2)}, u32[]{:S(2)}) collective-permute-start(f32[3,88,128]{2,1,0:T(8,128)S(1)} %collective-permute-done.12.o_ref), channel_id=1, source_target_pairs={{0,1},{1,0},{2,3},{3,2},{4,5},{5,4},{6,7},{7,6},{8,9},{9,8},{10,11... | collective-permute-start | bytes 405512 | tf_op jit(solution)/shard_map/ppermute | solution.py:397
  82.5 2.0 %collective-permute-start.14 = (f32[2,88,128]{2,1,0:T(8,128)S(1)}, f32[2,88,128]{2,1,0:T(8,128)S(1)}, u32[]{:S(2)}, u32[]{:S(2)}) collective-permute-start(f32[2,88,128]{2,1,0:T(8,128)S(1)} %get-tuple-element.162.rest_0_), channel_id=1, source_target_pairs={{0,1},{1,0},{2,3},{3,2},{4,5},{5,4},{6,7},{7,6},{8,9},{9,8},{10,11... | collective-permute-start | bytes 270344 | tf_op jit(solution)/shard_map/ppermute | solution.py:396
  87.2 4.8 %collective-permute-start.15 = (f32[3,88,128]{2,1,0:T(8,128)S(1)}, f32[3,88,128]{2,1,0:T(8,128)S(1)}, u32[]{:S(2)}, u32[]{:S(2)}) collective-permute-start(f32[3,88,128]{2,1,0:T(8,128)S(1)} %get-tuple-element.166.x_ref), channel_id=1, source_target_pairs={{1,2},{0,7},{3,4},{2,1},{5,6},{4,3},{7,0},{6,5},{9,10},{8,15},{11,... | collective-permute-start | bytes 405512 | tf_op jit(solution)/shard_map/ppermute | solution.py:390
  92.0 5.0 %collective-permute-start.16 = (f32[3,88,128]{2,1,0:T(8,128)S(1)}, f32[3,88,128]{2,1,0:T(8,128)S(1)}, u32[]{:S(2)}, u32[]{:S(2)}) collective-permute-start(f32[3,88,128]{2,1,0:T(8,128)S(1)} %collective-permute-done.15.o_ref), channel_id=1, source_target_pairs={{0,1},{1,0},{2,3},{3,2},{4,5},{5,4},{6,7},{7,6},{8,9},{9,8},{10,11... | collective-permute-start | bytes 405512 | tf_op jit(solution)/shard_map/ppermute | solution.py:397
  93.6 3.4 %collective-permute-start.17 = (f32[2,88,128]{2,1,0:T(8,128)S(1)}, f32[2,88,128]{2,1,0:T(8,128)S(1)}, u32[]{:S(2)}, u32[]{:S(2)}) collective-permute-start(f32[2,88,128]{2,1,0:T(8,128)S(1)} %get-tuple-element.178.rest_0_), channel_id=1, source_target_pairs={{0,1},{1,0},{2,3},{3,2},{4,5},{5,4},{6,7},{7,6},{8,9},{9,8},{10,11... | collective-permute-start | bytes 270344 | tf_op jit(solution)/shard_map/ppermute | solution.py:396
  99.7 4.9 %collective-permute-start.18 = (f32[3,88,128]{2,1,0:T(8,128)S(1)}, f32[3,88,128]{2,1,0:T(8,128)S(1)}, u32[]{:S(2)}, u32[]{:S(2)}) collective-permute-start(f32[3,88,128]{2,1,0:T(8,128)S(1)} %get-tuple-element.182.x_ref), channel_id=1, source_target_pairs={{1,2},{0,7},{3,4},{2,1},{5,6},{4,3},{7,0},{6,5},{9,10},{8,15},{11,... | collective-permute-start | bytes 405512 | tf_op jit(solution)/shard_map/ppermute | solution.py:390
  104.7 3.1 %collective-permute-start.19 = (f32[3,88,128]{2,1,0:T(8,128)S(1)}, f32[3,88,128]{2,1,0:T(8,128)S(1)}, u32[]{:S(2)}, u32[]{:S(2)}) collective-permute-start(f32[3,88,128]{2,1,0:T(8,128)S(1)} %collective-permute-done.18.o_ref), channel_id=1, source_target_pairs={{0,1},{1,0},{2,3},{3,2},{4,5},{5,4},{6,7},{7,6},{8,9},{9,8},{10,11... | collective-permute-start | bytes 405512 | tf_op jit(solution)/shard_map/ppermute | solution.py:397
  105.9 1.9 %collective-permute-start.20 = (f32[2,88,128]{2,1,0:T(8,128)S(1)}, f32[2,88,128]{2,1,0:T(8,128)S(1)}, u32[]{:S(2)}, u32[]{:S(2)}) collective-permute-start(f32[2,88,128]{2,1,0:T(8,128)S(1)} %get-tuple-element.194.rest_0_), channel_id=1, source_target_pairs={{0,1},{1,0},{2,3},{3,2},{4,5},{5,4},{6,7},{7,6},{8,9},{9,8},{10,11... | collective-permute-start | bytes 270344 | tf_op jit(solution)/shard_map/ppermute | solution.py:396
  110.8 4.4 %collective-permute-start.21 = (f32[3,88,128]{2,1,0:T(8,128)S(1)}, f32[3,88,128]{2,1,0:T(8,128)S(1)}, u32[]{:S(2)}, u32[]{:S(2)}) collective-permute-start(f32[3,88,128]{2,1,0:T(8,128)S(1)} %get-tuple-element.198.x_ref), channel_id=1, source_target_pairs={{1,2},{0,7},{3,4},{2,1},{5,6},{4,3},{7,0},{6,5},{9,10},{8,15},{11,... | collective-permute-start | bytes 405512 | tf_op jit(solution)/shard_map/ppermute | solution.py:410
  115.2 4.3 %collective-permute-start.22 = (f32[3,88,128]{2,1,0:T(8,128)S(1)}, f32[3,88,128]{2,1,0:T(8,128)S(1)}, u32[]{:S(2)}, u32[]{:S(2)}) collective-permute-start(f32[3,88,128]{2,1,0:T(8,128)S(1)} %collective-permute-done.21.o_ref), channel_id=1, source_target_pairs={{0,1},{1,0},{2,3},{3,2},{4,5},{5,4},{6,7},{7,6},{8,9},{9,8},{10,11... | collective-permute-start | bytes 405512 | tf_op jit(solution)/shard_map/ppermute | solution.py:413
where the time goes:
time: 128 us; the launch traced here: 130 us
  Pallas kernels  72.7 us (57%)
  starting transfers between devices  23.1 us (18%)
  blocking collectives  20.2 us (16%)
  waiting for transfers between devices  8 us (6%)
  local copies, waits for them, and re-layouts  4.62 us (4%)
    pallas_call x13, Pallas kernels, update(): return kernel(*inside(at, left, meta, tri, cell_pos, cells_now))  36.6 us
    all_to_all x1, blocking collectives, on_device(): lax.all_to_all(jnp.broadcast_to(block[None], (nbatch,) + block.shape), 'r...  20.2 us
    pallas_call x6, Pallas kernels, middle(): *packs, x, y = crit(*inside(x, y, o, e, near, far))  16.5 us
    pallas_call x6, Pallas kernels, middle(): near, rest = rows(jnp.full((1,), g + 1, jnp.int32), *inside(*packs, rest))  14.5 us
    ppermute x6, starting transfers between devices, middle(): e = lax.ppermute(o, 'tile', partner)  10.2 us
    ppermute x2, starting transfers between devices, on_device(): e = lax.ppermute(o, 'tile', partner)  4.81 us
    ppermute x2, waiting for transfers between devices, on_device(): o = lax.ppermute(x, 'tile', across)  3.39 us
    ppermute x6, starting transfers between devices, middle(): o = lax.ppermute(x, 'tile', across)  2.93 us
  transfers between devices with their start and end apart: 23, of which 9 were waited for; matrix products, arithmetic and copies ran while one was open for 0% of the time, Pallas kernels for 35%

commit v1 on v0

--- a/solution.py
+++ b/solution.py
@@ -8,7 +8,7 @@
 EPSILON = 1e-06
 META = 8
 WIDE = 256
-ROOM = 32 * 1024 * 1024
+ROOM = 16 * 1024 * 1024
 F32 = jnp.float32
 BF16 = jnp.bfloat16
 
@@ -100,6 +100,34 @@
 
 def inside(*arrays):
     return [pltpu.with_memory_space_constraint(a, pltpu.VMEM) for a in arrays]
+
+
+def make_prepare(members, slots, nbatch, tile_width):
+    full = members + META
+
+    def prepare(start_ref, count_ref, rows_ref, val_ref, noise_ref, cell_ref, class_ref, b_ref):
+        lane = lax.broadcasted_iota(jnp.int32, (1, slots), 1)
+        meta = [
+            val_ref[...],
+            noise_ref[...],
+            (cell_ref[...] + start_ref[0]).astype(F32),
+            (tile_width / 4) * (class_ref[...] + 2).astype(F32),
+            jnp.where(lane < count_ref[0, 0], 1.0, 0.0),
+            jnp.zeros((META - 5, slots), F32),
+        ]
+        meta = jnp.concatenate(meta, axis=0)
+        for b in range(nbatch):
+            b_ref[b, :members] = rows_ref[...]
+            b_ref[b, members:] = meta
+
+    smem = pl.BlockSpec(memory_space=pltpu.SMEM)
+    return pl.pallas_call(
+        prepare,
+        in_specs=[smem] * 2 + [pl.BlockSpec(memory_space=pltpu.VMEM)] * 5,
+        out_shape=vmem((nbatch, full, slots), F32),
+        compiler_params=pltpu.CompilerParams(vmem_limit_bytes=ROOM),
+        name="prepare",
+    )
 
 
 def make_crit(members, slots, last):
@@ -195,28 +223,27 @@
     lax.fori_loop(0, 2, one, 0)
 
 
-def make_rows(members, slots, groups):
+def make_rows(members, slots, groups, abreast):
     full = members + META
 
     def rows(begin_ref, *all_refs):
         *refs, r_ref, n_ref, ro_ref, zs_ref = all_refs
         begin = begin_ref[0]
 
-        def couple(c, carry):
+        def several(c, carry):
+            spots = [jnp.minimum(begin + abreast * c + i, groups - 1) for i in range(abreast)]
             tpos = []
-            for i in range(2):
-                q = begin + 2 * c + i
+            for i, q in enumerate(spots):
                 both = jnp.concatenate([ro_ref[q, 0], ro_ref[q, 1]], axis=1)
                 zs_ref[i] = both[:members]
                 tpos.append(both[members + 2 : members + 3])
             run_steps(zs_ref, tpos, refs, 0, slots)
-            for i in range(2):
-                q = begin + 2 * c + i
+            for i, q in enumerate(spots):
                 for k in range(2):
                     ro_ref[q, k, :members] = zs_ref[i, :, k * slots : (k + 1) * slots]
             return carry
 
-        lax.fori_loop(0, (groups - begin + 1) // 2, couple, 0)
+        lax.fori_loop(0, (groups - begin + abreast - 1) // abreast, several, 0)
         n_ref[...] = ro_ref[begin]
 
     smem = pl.BlockSpec(memory_space=pltpu.SMEM)
@@ -224,9 +251,9 @@
     return pl.pallas_call(
         rows,
         in_specs=[smem] + rest,
-        out_shape=(vmem((2, full, slots), F32), vmem((groups + 1, 2, full, slots), F32)),
+        out_shape=(vmem((2, full, slots), F32), vmem((groups, 2, full, slots), F32)),
         input_output_aliases={6: 1},
-        scratch_shapes=(pltpu.VMEM((2, members, 2 * slots), F32),),
+        scratch_shapes=(pltpu.VMEM((abreast, members, 2 * slots), F32),),
         compiler_params=pltpu.CompilerParams(vmem_limit_bytes=ROOM),
         name="rows",
     )
@@ -347,20 +374,14 @@
     cell_pos = (
         tile_index * tile_width + region_index * cells + jnp.arange(cells, dtype=jnp.int32)
     ).astype(F32)[None]
-    pos = (tile_index * tile_width + obs_cell[0, 0]).astype(F32)
-    half = (tile_width / 4) * (obs_class[0, 0] + 2).astype(F32)
-    live = (jnp.arange(slots, dtype=jnp.int32) < obs_count[0, 0]).astype(F32)
-    zero = jnp.zeros_like(pos)
-    block = jnp.concatenate(
-        [
-            obs_rows[0, :, 0, :],
-            jnp.stack([obs_value[0, 0], obs_noise[0, 0], pos, half, live, zero, zero, zero]),
-        ],
-        axis=0,
-    )
-    own = lax.all_to_all(
-        jnp.broadcast_to(block[None], (nbatch,) + block.shape), "region", 0, 0, tiled=True
-    )
+    prepare = make_prepare(members, slots, nbatch, tile_width)
+    copies = prepare(
+        jnp.full((1,), tile_index * tile_width, jnp.int32),
+        obs_count,
+        *(obs_rows[0, :, 0, :], obs_value[0], obs_noise[0], obs_cell[0], obs_class[0]),
+    )
+    own = lax.all_to_all(copies, "region", 0, 0, tiled=True)
+    block = own[0]
     partner = [(i, i ^ 1) for i in range(tiles)]
     across = []
     for z in range(chips):
@@ -372,7 +393,7 @@
     y = other[1]
     near = own[2:4]
     far = other[2:4]
-    rest = jnp.concatenate([own, jnp.zeros_like(own[:2])]).reshape(groups + 1, 2, *block.shape)
+    rest = own.reshape(groups, 2, *block.shape)
     cells_now = state[:, 0, :]
     order = jnp.arange(3 * slots, dtype=jnp.int32)
     tri = (order[:, None] < order[None, :]).astype(BF16)
@@ -383,7 +404,6 @@
         return kernel(*inside(at, left, meta, tri, cell_pos, cells_now))
 
     crit = make_crit(members, slots, False)
-    rows = make_rows(members, slots, groups)
 
     def middle(g, carry):
         x, y, rest, cells_now, *packs = carry
@@ -391,6 +411,8 @@
         if g > 2:
             cells_now = update((0,), packs, cells_now)
             o, cells_now = lax.optimization_barrier((o, cells_now))
+        left = groups - g - 1
+        rows = make_rows(members, slots, groups, left if left < 4 else 2 + left // 5)
         near, rest = rows(jnp.full((1,), g + 1, jnp.int32), *inside(*packs, rest))
         o, near = lax.optimization_barrier((o, near))
         far = lax.ppermute(near, "tile", partner)

time: 128 us -> 124 us (0.969); the launches traced: 130 us -> 122 us
  Pallas kernels: 72.7 us -> 64.7 us
  waiting for transfers between devices: 8 us -> 11.7 us
  starting transfers between devices: 23.1 us -> 21.4 us
  local copies, waits for them, and re-layouts: 4.62 us -> 3.21 us
    pallas_call x13, Pallas kernels: 36.6 us -> 31.1 us  [update(): return kernel(*inside(at, left, meta, tri, cell_pos, cells_now))]
    ppermute x6, starting transfers between devices: 2.93 us -> 6 us  [middle(): o = lax.ppermute(x, 'tile', across)]
    ppermute x6, starting transfers between devices: 10.2 us -> 7.27 us  [middle(): e = lax.ppermute(o, 'tile', partner)]
    pallas_call x6, Pallas kernels: 14.5 us -> 11.9 us  [middle(): near, rest = rows(jnp.full((1,), g + 1, jnp.int32), *inside(*packs, rest))]
    ppermute x2, waiting for transfers between devices: 3.39 us -> 5.64 us  [on_device(): o = lax.ppermute(x, 'tile', across)]
    ppermute x6, waiting for transfers between devices: 2.55 us -> 4.01 us  [middle(): o = lax.ppermute(x, 'tile', across)]
  transfers between devices with their start and end apart: 23 -> 23, of which waited for: 9 -> 7; matrix products, arithmetic and copies ran while one was open for 0% -> 0% of each run, Pallas kernels for 35% -> 32%
where the time goes in v1:
time: 124 us; the launch traced here: 122 us
  Pallas kernels  64.7 us (52%)
  starting transfers between devices  21.4 us (17%)
  blocking collectives  20.2 us (16%)
  waiting for transfers between devices  11.7 us (9%)
  local copies, waits for them, and re-layouts  3.21 us (3%)
    pallas_call x13, Pallas kernels, update(): return kernel(*inside(at, left, meta, tri, cell_pos, cells_now))  31.1 us
    all_to_all x1, blocking collectives, on_device(): own = lax.all_to_all(copies, 'region', 0, 0, tiled=True)  20.2 us
    pallas_call x6, Pallas kernels, middle(): *packs, x, y = crit(*inside(x, y, o, e, near, far))  16.5 us
    pallas_call x6, Pallas kernels, middle(): near, rest = rows(jnp.full((1,), g + 1, jnp.int32), *inside(*packs, rest))  11.9 us
    ppermute x6, starting transfers between devices, middle(): e = lax.ppermute(o, 'tile', partner)  7.27 us
    ppermute x6, starting transfers between devices, middle(): o = lax.ppermute(x, 'tile', across)  6 us
    ppermute x2, waiting for transfers between devices, on_device(): o = lax.ppermute(x, 'tile', across)  5.64 us
    ppermute x6, waiting for transfers between devices, middle(): o = lax.ppermute(x, 'tile', across)  4.01 us
  transfers between devices with their start and end apart: 23, of which 7 were waited for; matrix products, arithmetic and copies ran while one was open for 0% of the time, Pallas kernels for 32%

profile of v1, /device:TPU:1, one launch (start us, length us, event | category | flops | bytes accessed | tf_op | source)
XLA Modules:
  0.0 122.3 jit_solution(4727500443561664772)
XLA Ops:
  1.4 0.8 copy-done
  2.2 20.2 %all_to_all.5 = f32[16,88,128]{2,1,0:T(8,128)S(1)} all-to-all(f32[16,88,128]{2,1,0:T(8,128)S(1)} %prepare.1), channel_id=1, replica_groups=mesh['region'=16,'tile'=8] {'region'}, dimensions={0} | all-to-all | bytes 1441792 | tf_op jit(solution)/shard_map/all_to_all | solution.py:383
  22.4 1.9 %collective-permute-start = (f32[4,88,128]{2,1,0:T(8,128)S(1)}, f32[4,88,128]{2,1,0:T(8,128)S(1)}, u32[]{:S(2)}, u32[]{:S(2)}) collective-permute-start(f32[4,88,128]{2,1,0:T(8,128)S(1)} %slice.29), channel_id=1, source_target_pairs={{0,1},{1,0},{2,3},{3,2},{4,5},{5,4},{6,7},{7,6},{8,9},{9,8},{10,11... | collective-permute-start | bytes 540680 | tf_op jit(solution)/shard_map/ppermute | solution.py:391
  24.3 1.0 collective-permute-done
  25.3 2.0 %collective-permute-start.1 = (f32[3,88,128]{2,1,0:T(8,128)S(1)}, f32[3,88,128]{2,1,0:T(8,128)S(1)}, u32[]{:S(2)}, u32[]{:S(2)}) collective-permute-start(f32[3,88,128]{2,1,0:T(8,128)S(1)} %pad_maximum_fusion.x_ref), channel_id=1, source_target_pairs={{1,2},{0,7},{3,4},{2,1},{5,6},{4,3},{7,0},{6,5},{9,10},{8,15},{11,... | collective-permute-start | bytes 405512 | tf_op jit(solution)/shard_map/ppermute | solution.py:425
  27.3 2.7 %collective-permute-done.1.o_ref = f32[3,88,128]{2,1,0:T(8,128)S(1)} collective-permute-done((f32[3,88,128]{2,1,0:T(8,128)S(1)}, f32[3,88,128]{2,1,0:T(8,128)S(1)}, u32[]{:S(2)}, u32[]{:S(2)}) %collective-permute-start.1) | collective-permute-done | bytes 135200 | tf_op jit(solution)/shard_map/ppermute | solution.py:425
  30.0 2.3 %collective-permute-start.2 = (f32[3,88,128]{2,1,0:T(8,128)S(1)}, f32[3,88,128]{2,1,0:T(8,128)S(1)}, u32[]{:S(2)}, u32[]{:S(2)}) collective-permute-start(f32[3,88,128]{2,1,0:T(8,128)S(1)} %collective-permute-done.1.o_ref), channel_id=1, source_target_pairs={{0,1},{1,0},{2,3},{3,2},{4,5},{5,4},{6,7},{7,6},{8,9},{9,8},{10,11... | collective-permute-start | bytes 405512 | tf_op jit(solution)/shard_map/ppermute | solution.py:426
  32.3 1.0 collective-permute-done.2.e_ref
  33.2 2.6 %crit.8 = (bf16[2,512,256]{2,1,0:T(8,128)(2,1)S(1)}, bf16[2,160,1024]{2,1,0:T(8,128)(2,1)S(1)}, f32[2,4,128,128]{3,2,1,0:T(8,128)S(1)}, f32[2,4,128,128]{3,2,1,0...) custom-call(f32[3,88,128]{2,1,0:T(8,128)S(1)} %pad_maximum_fusion.x_ref, ...), custom_call_target="tpu_custom_call" | custom-call | tf_op jit(solution)/shard_map/crit/pallas_call | solution.py:427
  36.0 2.9 %rows.6 = (f32[2,88,128]{2,1,0:T(8,128)S(1)}, f32[8,2,88,128]{3,2,1,0:T(8,128)S(1)}) custom-call(s32[1]{0:T(128)} %constant.5.clone.1.begin_ref, bf16[2,512,256]{2,1,0:T(8,128)(2,1)S(1)} %get-tuple-element.110.all_refs_0_, bf16[2,160,1024]{2,1,0:T(8,128)(2,1)S(1)} %get-tuple-element.111.all_refs_1_, ...), custom_call_target="tpu_custom_call", output_to_operand_aliasing={{1}: (6, {})} | custom-call | tf_op jit(solution)/shard_map/rows/pallas_call | solution.py:416
  38.9 1.8 %collective-permute-done.3.o_ref = f32[3,88,128]{2,1,0:T(8,128)S(1)} collective-permute-done((f32[3,88,128]{2,1,0:T(8,128)S(1)}, f32[3,88,128]{2,1,0:T(8,128)S(1)}, u32[]{:S(2)}, u32[]{:S(2)}) %collective-permute-start.3) | collective-permute-done | bytes 135200 | tf_op jit(solution)/shard_map/ppermute | solution.py:410
  40.7 1.5 %collective-permute-start.4 = (f32[3,88,128]{2,1,0:T(8,128)S(1)}, f32[3,88,128]{2,1,0:T(8,128)S(1)}, u32[]{:S(2)}, u32[]{:S(2)}) collective-permute-start(f32[3,88,128]{2,1,0:T(8,128)S(1)} %collective-permute-done.3.o_ref), channel_id=1, source_target_pairs={{0,1},{1,0},{2,3},{3,2},{4,5},{5,4},{6,7},{7,6},{8,9},{9,8},{10,11... | collective-permute-start | bytes 405512 | tf_op jit(solution)/shard_map/ppermute | solution.py:419
  42.6 3.5 %cells.13.all_refs_5_ = f32[80,2048]{1,0:T(8,128)S(1)} custom-call(bf16[2,512,256]{2,1,0:T(8,128)(2,1)S(1)} %get-tuple-element.110.all_refs_0_, bf16[2,160,1024]{2,1,0:T(8,128)(2,1)S(1)} %get-tuple-element.111.all_refs_1_, f32[2,8,512]{2,1,0:T(8,128)S(1)} %get-tuple-element.114.all_refs_4_.all_refs_2_, ...), custom_call_target="tpu_custom_call", output_to_operand_aliasing={{}: (5, {})} | custom-call | tf_op jit(solution)/shard_map/cells/pallas_call | solution.py:404
  46.1 2.7 %crit.9 = (bf16[2,512,256]{2,1,0:T(8,128)(2,1)S(1)}, bf16[2,160,1024]{2,1,0:T(8,128)(2,1)S(1)}, f32[2,4,128,128]{3,2,1,0:T(8,128)S(1)}, f32[2,4,128,128]{3,2,1,0...) custom-call(f32[3,88,128]{2,1,0:T(8,128)S(1)} %get-tuple-element.108.x_ref, ...), custom_call_target="tpu_custom_call" | custom-call | tf_op jit(solution)/shard_map/crit/pallas_call | solution.py:422
  48.8 1.6 %collective-permute-start.6 = (f32[3,88,128]{2,1,0:T(8,128)S(1)}, f32[3,88,128]{2,1,0:T(8,128)S(1)}, u32[]{:S(2)}, u32[]{:S(2)}) collective-permute-start(f32[3,88,128]{2,1,0:T(8,128)S(1)} %get-tuple-element.120.x_ref), channel_id=1, source_target_pairs={{1,2},{0,7},{3,4},{2,1},{5,6},{4,3},{7,0},{6,5},{9,10},{8,15},{11,... | collective-permute-start | bytes 405512 | tf_op jit(solution)/shard_map/ppermute | solution.py:410
  50.5 3.0 %rows.7 = (f32[2,88,128]{2,1,0:T(8,128)S(1)}, f32[8,2,88,128]{3,2,1,0:T(8,128)S(1)}) custom-call(s32[1]{0:T(128)} %constant.9.clone.1.begin_ref, bf16[2,512,256]{2,1,0:T(8,128)(2,1)S(1)} %get-tuple-element.122.all_refs_0_, bf16[2,160,1024]{2,1,0:T(8,128)(2,1)S(1)} %get-tuple-element.123.all_refs_1_, ...), custom_call_target="tpu_custom_call", output_to_operand_aliasing={{1}: (6, {})} | custom-call | tf_op jit(solution)/shard_map/rows/pallas_call | solution.py:416
  53.7 1.5 %collective-permute-start.7 = (f32[3,88,128]{2,1,0:T(8,128)S(1)}, f32[3,88,128]{2,1,0:T(8,128)S(1)}, u32[]{:S(2)}, u32[]{:S(2)}) collective-permute-start(f32[3,88,128]{2,1,0:T(8,128)S(1)} %collective-permute-done.6.o_ref), channel_id=1, source_target_pairs={{0,1},{1,0},{2,3},{3,2},{4,5},{5,4},{6,7},{7,6},{8,9},{9,8},{10,11... | collective-permute-start | bytes 405512 | tf_op jit(solution)/shard_map/ppermute | solution.py:419
  55.3 4.8 %cells.14.all_refs_5_ = f32[80,2048]{1,0:T(8,128)S(1)} custom-call(bf16[2,512,256]{2,1,0:T(8,128)(2,1)S(1)} %get-tuple-element.122.all_refs_0_, bf16[2,160,1024]{2,1,0:T(8,128)(2,1)S(1)} %get-tuple-element.123.all_refs_1_, f32[2,8,512]{2,1,0:T(8,128)S(1)} %get-tuple-element.126.all_refs_4_.all_refs_2_, ...), custom_call_target="tpu_custom_call", output_to_operand_aliasing={{}: (5, {})} | custom-call | tf_op jit(solution)/shard_map/cells/pallas_call | solution.py:404
  60.2 2.7 %crit.10 = (bf16[2,512,256]{2,1,0:T(8,128)(2,1)S(1)}, bf16[2,160,1024]{2,1,0:T(8,128)(2,1)S(1)}, f32[2,4,128,128]{3,2,1,0:T(8,128)S(1)}, f32[2,4,128,128]{3,2,1,...) custom-call(f32[3,88,128]{2,1,0:T(8,128)S(1)} %get-tuple-element.120.x_ref, ...), custom_call_target="tpu_custom_call" | custom-call | tf_op jit(solution)/shard_map/crit/pallas_call | solution.py:422
  62.9 1.7 %collective-permute-start.9 = (f32[3,88,128]{2,1,0:T(8,128)S(1)}, f32[3,88,128]{2,1,0:T(8,128)S(1)}, u32[]{:S(2)}, u32[]{:S(2)}) collective-permute-start(f32[3,88,128]{2,1,0:T(8,128)S(1)} %get-tuple-element.134.x_ref), channel_id=1, source_target_pairs={{1,2},{0,7},{3,4},{2,1},{5,6},{4,3},{7,0},{6,5},{9,10},{8,15},{11,... | collective-permute-start | bytes 405512 | tf_op jit(solution)/shard_map/ppermute | solution.py:410
  64.6 1.8 %cells.15.all_refs_5_ = f32[80,2048]{1,0:T(8,128)S(1)} custom-call(bf16[2,512,256]{2,1,0:T(8,128)(2,1)S(1)} %get-tuple-element.136.all_refs_0_, bf16[2,160,1024]{2,1,0:T(8,128)(2,1)S(1)} %get-tuple-element.137.all_refs_1_, f32[2,8,512]{2,1,0:T(8,128)S(1)} %get-tuple-element.138.all_refs_2_.all_refs_4_, ...), custom_call_target="tpu_custom_call", output_to_operand_aliasing={{}: (5, {})} | custom-call | tf_op jit(solution)/shard_map/cells/pallas_call | solution.py:404
  66.4 2.4 %rows.8 = (f32[2,88,128]{2,1,0:T(8,128)S(1)}, f32[8,2,88,128]{3,2,1,0:T(8,128)S(1)}) custom-call(s32[1]{0:T(128)} %constant.10.clone.1.begin_ref, bf16[2,512,256]{2,1,0:T(8,128)(2,1)S(1)} %get-tuple-element.136.all_refs_0_, bf16[2,160,1024]{2,1,0:T(8,128)(2,1)S(1)} %get-tuple-element.137.all_refs_1_, ...), custom_call_target="tpu_custom_call", output_to_operand_aliasing={{1}: (6, {})} | custom-call | tf_op jit(solution)/shard_map/rows/pallas_call | solution.py:416
  69.4 1.8 %cells.16.all_refs_5_ = f32[80,2048]{1,0:T(8,128)S(1)} custom-call(bf16[2,512,256]{2,1,0:T(8,128)(2,1)S(1)} %get-tuple-element.136.all_refs_0_, bf16[2,160,1024]{2,1,0:T(8,128)(2,1)S(1)} %get-tuple-element.137.all_refs_1_, f32[2,8,512]{2,1,0:T(8,128)S(1)} %get-tuple-element.138.all_refs_2_.all_refs_4_, ...), custom_call_target="tpu_custom_call", output_to_operand_aliasing={{}: (5, {})} | custom-call | tf_op jit(solution)/shard_map/cells/pallas_call | solution.py:404
  71.2 2.7 %crit.11 = (bf16[2,512,256]{2,1,0:T(8,128)(2,1)S(1)}, bf16[2,160,1024]{2,1,0:T(8,128)(2,1)S(1)}, f32[2,4,128,128]{3,2,1,0:T(8,128)S(1)}, f32[2,4,128,128]{3,2,1,...) custom-call(f32[3,88,128]{2,1,0:T(8,128)S(1)} %get-tuple-element.134.x_ref, ...), custom_call_target="tpu_custom_call" | custom-call | tf_op jit(solution)/shard_map/crit/pallas_call | solution.py:422
  73.9 1.7 %collective-permute-start.12 = (f32[3,88,128]{2,1,0:T(8,128)S(1)}, f32[3,88,128]{2,1,0:T(8,128)S(1)}, u32[]{:S(2)}, u32[]{:S(2)}) collective-permute-start(f32[3,88,128]{2,1,0:T(8,128)S(1)} %get-tuple-element.150.x_ref), channel_id=1, source_target_pairs={{1,2},{0,7},{3,4},{2,1},{5,6},{4,3},{7,0},{6,5},{9,10},{8,15},{11,... | collective-permute-start | bytes 405512 | tf_op jit(solution)/shard_map/ppermute | solution.py:410
  75.6 1.8 %cells.17.all_refs_5_ = f32[80,2048]{1,0:T(8,128)S(1)} custom-call(bf16[2,512,256]{2,1,0:T(8,128)(2,1)S(1)} %get-tuple-element.152.all_refs_0_, bf16[2,160,1024]{2,1,0:T(8,128)(2,1)S(1)} %get-tuple-element.153.all_refs_1_, f32[2,8,512]{2,1,0:T(8,128)S(1)} %get-tuple-element.154.all_refs_2_.all_refs_4_, ...), custom_call_target="tpu_custom_call", output_to_operand_aliasing={{}: (5, {})} | custom-call | tf_op jit(solution)/shard_map/cells/pallas_call | solution.py:404
  77.4 1.5 %rows.9 = (f32[2,88,128]{2,1,0:T(8,128)S(1)}, f32[8,2,88,128]{3,2,1,0:T(8,128)S(1)}) custom-call(s32[1]{0:T(128)} %constant.22.clone.1.begin_ref, bf16[2,512,256]{2,1,0:T(8,128)(2,1)S(1)} %get-tuple-element.152.all_refs_0_, bf16[2,160,1024]{2,1,0:T(8,128)(2,1)S(1)} %get-tuple-element.153.all_refs_1_, ...), custom_call_target="tpu_custom_call", output_to_operand_aliasing={{1}: (6, {})} | custom-call | tf_op jit(solution)/shard_map/rows/pallas_call | solution.py:416
  78.9 1.0 collective-permute-start.13
  79.8 1.8 %cells.18.all_refs_5_ = f32[80,2048]{1,0:T(8,128)S(1)} custom-call(bf16[2,512,256]{2,1,0:T(8,128)(2,1)S(1)} %get-tuple-element.152.all_refs_0_, bf16[2,160,1024]{2,1,0:T(8,128)(2,1)S(1)} %get-tuple-element.153.all_refs_1_, f32[2,8,512]{2,1,0:T(8,128)S(1)} %get-tuple-element.154.all_refs_2_.all_refs_4_, ...), custom_call_target="tpu_custom_call", output_to_operand_aliasing={{}: (5, {})} | custom-call | tf_op jit(solution)/shard_map/cells/pallas_call | solution.py:404
  81.6 2.7 %crit.12 = (bf16[2,512,256]{2,1,0:T(8,128)(2,1)S(1)}, bf16[2,160,1024]{2,1,0:T(8,128)(2,1)S(1)}, f32[2,4,128,128]{3,2,1,0:T(8,128)S(1)}, f32[2,4,128,128]{3,2,1,...) custom-call(f32[3,88,128]{2,1,0:T(8,128)S(1)} %get-tuple-element.150.x_ref, ...), custom_call_target="tpu_custom_call" | custom-call | tf_op jit(solution)/shard_map/crit/pallas_call | solution.py:422
  85.1 3.1 %cells.19.all_refs_5_ = f32[80,2048]{1,0:T(8,128)S(1)} custom-call(bf16[2,512,256]{2,1,0:T(8,128)(2,1)S(1)} %get-tuple-element.168.all_refs_0_, bf16[2,160,1024]{2,1,0:T(8,128)(2,1)S(1)} %get-tuple-element.169.all_refs_1_, f32[2,8,512]{2,1,0:T(8,128)S(1)} %get-tuple-element.170.all_refs_2_.all_refs_4_, ...), custom_call_target="tpu_custom_call", output_to_operand_aliasing={{}: (5, {})} | custom-call | tf_op jit(solution)/shard_map/cells/pallas_call | solution.py:404
  88.2 1.2 %rows.10 = (f32[2,88,128]{2,1,0:T(8,128)S(1)}, f32[8,2,88,128]{3,2,1,0:T(8,128)S(1)}) custom-call(s32[1]{0:T(128)} %constant.23.clone.1.begin_ref, bf16[2,512,256]{2,1,0:T(8,128)(2,1)S(1)} %get-tuple-element.168.all_refs_0_, bf16[2,160,1024]{2,1,0:T(8,128)(2,1)S(1)} %get-tuple-element.169.all_refs_1_, ...), custom_call_target="tpu_custom_call", output_to_operand_aliasing={{1}: (6, {})} | custom-call | tf_op jit(solution)/shard_map/rows/pallas_call | solution.py:416
  89.4 1.6 %collective-permute-start.16 = (f32[3,88,128]{2,1,0:T(8,128)S(1)}, f32[3,88,128]{2,1,0:T(8,128)S(1)}, u32[]{:S(2)}, u32[]{:S(2)}) collective-permute-start(f32[3,88,128]{2,1,0:T(8,128)S(1)} %collective-permute-done.15.o_ref), channel_id=1, source_target_pairs={{0,1},{1,0},{2,3},{3,2},{4,5},{5,4},{6,7},{7,6},{8,9},{9,8},{10,11... | collective-permute-start | bytes 405512 | tf_op jit(solution)/shard_map/ppermute | solution.py:419
  91.2 2.0 %cells.20.all_refs_5_ = f32[80,2048]{1,0:T(8,128)S(1)} custom-call(bf16[2,512,256]{2,1,0:T(8,128)(2,1)S(1)} %get-tuple-element.168.all_refs_0_, bf16[2,160,1024]{2,1,0:T(8,128)(2,1)S(1)} %get-tuple-element.169.all_refs_1_, f32[2,8,512]{2,1,0:T(8,128)S(1)} %get-tuple-element.170.all_refs_2_.all_refs_4_, ...), custom_call_target="tpu_custom_call", output_to_operand_aliasing={{}: (5, {})} | custom-call | tf_op jit(solution)/shard_map/cells/pallas_call | solution.py:404
  93.2 2.7 %crit.13 = (bf16[2,512,256]{2,1,0:T(8,128)(2,1)S(1)}, bf16[2,160,1024]{2,1,0:T(8,128)(2,1)S(1)}, f32[2,4,128,128]{3,2,1,0:T(8,128)S(1)}, f32[2,4,128,128]{3,2,1,...) custom-call(f32[3,88,128]{2,1,0:T(8,128)S(1)} %get-tuple-element.166.x_ref, ...), custom_call_target="tpu_custom_call" | custom-call | tf_op jit(solution)/shard_map/crit/pallas_call | solution.py:422
  96.0 1.8 %cells.21.all_refs_5_ = f32[80,2048]{1,0:T(8,128)S(1)} custom-call(bf16[2,512,256]{2,1,0:T(8,128)(2,1)S(1)} %get-tuple-element.184.all_refs_0_, bf16[2,160,1024]{2,1,0:T(8,128)(2,1)S(1)} %get-tuple-element.185.all_refs_1_, f32[2,8,512]{2,1,0:T(8,128)S(1)} %get-tuple-element.186.all_refs_2_.all_refs_4_, ...), custom_call_target="tpu_custom_call", output_to_operand_aliasing={{}: (5, {})} | custom-call | tf_op jit(solution)/shard_map/cells/pallas_call | solution.py:404
  97.8 1.0 rows.11
  98.7 2.0 %collective-permute-done.18.o_ref = f32[3,88,128]{2,1,0:T(8,128)S(1)} collective-permute-done((f32[3,88,128]{2,1,0:T(8,128)S(1)}, f32[3,88,128]{2,1,0:T(8,128)S(1)}, u32[]{:S(2)}, u32[]{:S(2)}) %collective-permute-start.18) | collective-permute-done | bytes 135200 | tf_op jit(solution)/shard_map/ppermute | solution.py:410
  100.7 1.3 %collective-permute-start.19 = (f32[3,88,128]{2,1,0:T(8,128)S(1)}, f32[3,88,128]{2,1,0:T(8,128)S(1)}, u32[]{:S(2)}, u32[]{:S(2)}) collective-permute-start(f32[3,88,128]{2,1,0:T(8,128)S(1)} %collective-permute-done.18.o_ref), channel_id=1, source_target_pairs={{0,1},{1,0},{2,3},{3,2},{4,5},{5,4},{6,7},{7,6},{8,9},{9,8},{10,11... | collective-permute-start | bytes 405512 | tf_op jit(solution)/shard_map/ppermute | solution.py:419
  102.0 1.8 %cells.22.all_refs_5_ = f32[80,2048]{1,0:T(8,128)S(1)} custom-call(bf16[2,512,256]{2,1,0:T(8,128)(2,1)S(1)} %get-tuple-element.184.all_refs_0_, bf16[2,160,1024]{2,1,0:T(8,128)(2,1)S(1)} %get-tuple-element.185.all_refs_1_, f32[2,8,512]{2,1,0:T(8,128)S(1)} %get-tuple-element.186.all_refs_2_.all_refs_4_, ...), custom_call_target="tpu_custom_call", output_to_operand_aliasing={{}: (5, {})} | custom-call | tf_op jit(solution)/shard_map/cells/pallas_call | solution.py:404
  103.8 3.1 %crit.14 = (bf16[2,512,256]{2,1,0:T(8,128)(2,1)S(1)}, bf16[2,160,1024]{2,1,0:T(8,128)(2,1)S(1)}, f32[2,4,128,128]{3,2,1,0:T(8,128)}, f32[2,4,128,128]{3,2,1,0:T(...) custom-call(f32[3,88,128]{2,1,0:T(8,128)S(1)} %get-tuple-element.182.x_ref, ...), custom_call_target="tpu_custom_call" | custom-call | tf_op jit(solution)/shard_map/crit/pallas_call | solution.py:422
  106.9 1.8 %cells.23.all_refs_5_ = f32[80,2048]{1,0:T(8,128)S(1)} custom-call(bf16[2,512,256]{2,1,0:T(8,128)(2,1)S(1)} %get-tuple-element.200.all_refs_0_, bf16[2,160,1024]{2,1,0:T(8,128)(2,1)S(1)} %get-tuple-element.201.all_refs_1_, f32[2,8,512]{2,1,0:T(8,128)S(1)} %get-tuple-element.202.all_refs_2_, ...), custom_call_target="tpu_custom_call", output_to_operand_aliasing={{}: (5, {})} | custom-call | tf_op jit(solution)/shard_map/cells/pallas_call | solution.py:404
  108.7 2.9 %collective-permute-done.21.o_ref = f32[3,88,128]{2,1,0:T(8,128)S(1)} collective-permute-done((f32[3,88,128]{2,1,0:T(8,128)S(1)}, f32[3,88,128]{2,1,0:T(8,128)S(1)}, u32[]{:S(2)}, u32[]{:S(2)}) %collective-permute-start.21) | collective-permute-done | bytes 135200 | tf_op jit(solution)/shard_map/ppermute | solution.py:432
  111.6 1.4 %collective-permute-start.22 = (f32[3,88,128]{2,1,0:T(8,128)S(1)}, f32[3,88,128]{2,1,0:T(8,128)S(1)}, u32[]{:S(2)}, u32[]{:S(2)}) collective-permute-start(f32[3,88,128]{2,1,0:T(8,128)S(1)} %collective-permute-done.21.o_ref), channel_id=1, source_target_pairs={{0,1},{1,0},{2,3},{3,2},{4,5},{5,4},{6,7},{7,6},{8,9},{9,8},{10,11... | collective-permute-start | bytes 405512 | tf_op jit(solution)/shard_map/ppermute | solution.py:435
  113.1 1.8 %cells.24.all_refs_5_ = f32[80,2048]{1,0:T(8,128)S(1)} custom-call(bf16[2,512,256]{2,1,0:T(8,128)(2,1)S(1)} %get-tuple-element.200.all_refs_0_, bf16[2,160,1024]{2,1,0:T(8,128)(2,1)S(1)} %get-tuple-element.201.all_refs_1_, f32[2,8,512]{2,1,0:T(8,128)S(1)} %get-tuple-element.202.all_refs_2_, ...), custom_call_target="tpu_custom_call", output_to_operand_aliasing={{}: (5, {})} | custom-call | tf_op jit(solution)/shard_map/cells/pallas_call | solution.py:404
  114.9 2.4 %crit.15 = (bf16[2,512,256]{2,1,0:T(8,128)(2,1)S(1)}, bf16[2,160,1024]{2,1,0:T(8,128)(2,1)S(1)}, f32[2,4,128,128]{3,2,1,0:T(8,128)}, f32[2,4,128,128]{3,2,1,0:T(8,128)}, f32[2,8,512]{2,1,0:T(8,128)S(1)}) custom-call(f32[3,88,128]{2,1,0:T(8,128)S(1)} %get-tuple-element.198.x_ref, f32[88,128]{1,0:T(8,128)S(1)} %get-tuple-element.199.y_ref, ...), custom_call_target="tpu_custom_call" | custom-call | tf_op jit(solution)/shard_map/crit/pallas_call | solution.py:438
  117.3 3.5 %cells.25 = f32[80,2048]{1,0:T(8,128)S(1)} custom-call(bf16[2,512,256]{2,1,0:T(8,128)(2,1)S(1)} %get-tuple-element.207.all_refs_0_, bf16[2,160,1024]{2,1,0:T(8,128)(2,1)S(1)} %get-tuple-element.208.all_refs_1_, f32[2,8,512]{2,1,0:T(8,128)S(1)} %get-tuple-element.209.all_refs_2_, ...), custom_call_target="tpu_custom_call", output_to_operand_aliasing={{}: (5, {})} | custom-call | tf_op jit(solution)/shard_map/cells/pallas_call | solution.py:404
  120.8 1.5 %copy.27 = f32[80,1,2048]{2,1,0:T(1,128)} copy(f32[80,1,2048]{2,0,1:T(8,128)S(1)} %bitcast.14) | data formatting | bytes 1310720 | tf_op jit(solution)/shard_map/broadcast_in_dim | solution.py:440
  (49 shorter events, 3.1 us)
Async XLA Ops:
  0.7 0.7 copy-start.4
  0.7 0.7 copy-start.1
  0.7 0.7 copy-start.2
  0.7 0.7 copy-start.3
  1.4 0.8 copy-start
  22.4 2.9 %collective-permute-start = (f32[4,88,128]{2,1,0:T(8,128)S(1)}, f32[4,88,128]{2,1,0:T(8,128)S(1)}, u32[]{:S(2)}, u32[]{:S(2)}) collective-permute-start(f32[4,88,128]{2,1,0:T(8,128)S(1)} %slice.29), channel_id=1, source_target_pairs={{0,1},{1,0},{2,3},{3,2},{4,5},{5,4},{6,7},{7,6},{8,9},{9,8},{10,11... | collective-permute-start | bytes 540680 | tf_op jit(solution)/shard_map/ppermute | solution.py:391
  25.3 4.7 %collective-permute-start.1 = (f32[3,88,128]{2,1,0:T(8,128)S(1)}, f32[3,88,128]{2,1,0:T(8,128)S(1)}, u32[]{:S(2)}, u32[]{:S(2)}) collective-permute-start(f32[3,88,128]{2,1,0:T(8,128)S(1)} %pad_maximum_fusion.x_ref), channel_id=1, source_target_pairs={{1,2},{0,7},{3,4},{2,1},{5,6},{4,3},{7,0},{6,5},{9,10},{8,15},{11,... | collective-permute-start | bytes 405512 | tf_op jit(solution)/shard_map/ppermute | solution.py:425
  30.0 3.3 %collective-permute-start.2 = (f32[3,88,128]{2,1,0:T(8,128)S(1)}, f32[3,88,128]{2,1,0:T(8,128)S(1)}, u32[]{:S(2)}, u32[]{:S(2)}) collective-permute-start(f32[3,88,128]{2,1,0:T(8,128)S(1)} %collective-permute-done.1.o_ref), channel_id=1, source_target_pairs={{0,1},{1,0},{2,3},{3,2},{4,5},{5,4},{6,7},{7,6},{8,9},{9,8},{10,11... | collective-permute-start | bytes 405512 | tf_op jit(solution)/shard_map/ppermute | solution.py:426
  35.9 4.8 %collective-permute-start.3 = (f32[3,88,128]{2,1,0:T(8,128)S(1)}, f32[3,88,128]{2,1,0:T(8,128)S(1)}, u32[]{:S(2)}, u32[]{:S(2)}) collective-permute-start(f32[3,88,128]{2,1,0:T(8,128)S(1)} %get-tuple-element.108.x_ref), channel_id=1, source_target_pairs={{1,2},{0,7},{3,4},{2,1},{5,6},{4,3},{7,0},{6,5},{9,10},{8,15},{11,... | collective-permute-start | bytes 405512 | tf_op jit(solution)/shard_map/ppermute | solution.py:410
  36.0 6.2 %copy-start.5 = (f32[80,1,2048]{2,1,0:T(1,128)S(1)}, f32[80,1,2048]{2,1,0:T(1,128)}, u32[]{:S(2)}) copy-start(f32[80,1,2048]{2,1,0:T(1,128)} %param.7) | copy-start | bytes 1966084
  40.7 5.4 %collective-permute-start.4 = (f32[3,88,128]{2,1,0:T(8,128)S(1)}, f32[3,88,128]{2,1,0:T(8,128)S(1)}, u32[]{:S(2)}, u32[]{:S(2)}) collective-permute-start(f32[3,88,128]{2,1,0:T(8,128)S(1)} %collective-permute-done.3.o_ref), channel_id=1, source_target_pairs={{0,1},{1,0},{2,3},{3,2},{4,5},{5,4},{6,7},{7,6},{8,9},{9,8},{10,11... | collective-permute-start | bytes 405512 | tf_op jit(solution)/shard_map/ppermute | solution.py:419
  42.5 3.7 %collective-permute-start.5 = (f32[2,88,128]{2,1,0:T(8,128)S(1)}, f32[2,88,128]{2,1,0:T(8,128)S(1)}, u32[]{:S(2)}, u32[]{:S(2)}) collective-permute-start(f32[2,88,128]{2,1,0:T(8,128)S(1)} %get-tuple-element.117.rest_0_), channel_id=1, source_target_pairs={{0,1},{1,0},{2,3},{3,2},{4,5},{5,4},{6,7},{7,6},{8,9},{9,8},{10,11... | collective-permute-start | bytes 270344 | tf_op jit(solution)/shard_map/ppermute | solution.py:418
  48.8 4.8 %collective-permute-start.6 = (f32[3,88,128]{2,1,0:T(8,128)S(1)}, f32[3,88,128]{2,1,0:T(8,128)S(1)}, u32[]{:S(2)}, u32[]{:S(2)}) collective-permute-start(f32[3,88,128]{2,1,0:T(8,128)S(1)} %get-tuple-element.120.x_ref), channel_id=1, source_target_pairs={{1,2},{0,7},{3,4},{2,1},{5,6},{4,3},{7,0},{6,5},{9,10},{8,15},{11,... | collective-permute-start | bytes 405512 | tf_op jit(solution)/shard_map/ppermute | solution.py:410
  53.7 6.5 %collective-permute-start.7 = (f32[3,88,128]{2,1,0:T(8,128)S(1)}, f32[3,88,128]{2,1,0:T(8,128)S(1)}, u32[]{:S(2)}, u32[]{:S(2)}) collective-permute-start(f32[3,88,128]{2,1,0:T(8,128)S(1)} %collective-permute-done.6.o_ref), channel_id=1, source_target_pairs={{0,1},{1,0},{2,3},{3,2},{4,5},{5,4},{6,7},{7,6},{8,9},{9,8},{10,11... | collective-permute-start | bytes 405512 | tf_op jit(solution)/shard_map/ppermute | solution.py:419
  55.2 4.9 %collective-permute-start.8 = (f32[2,88,128]{2,1,0:T(8,128)S(1)}, f32[2,88,128]{2,1,0:T(8,128)S(1)}, u32[]{:S(2)}, u32[]{:S(2)}) collective-permute-start(f32[2,88,128]{2,1,0:T(8,128)S(1)} %get-tuple-element.130.rest_0_), channel_id=1, source_target_pairs={{0,1},{1,0},{2,3},{3,2},{4,5},{5,4},{6,7},{7,6},{8,9},{9,8},{10,11... | collective-permute-start | bytes 270344 | tf_op jit(solution)/shard_map/ppermute | solution.py:418
  62.9 6.0 %collective-permute-start.9 = (f32[3,88,128]{2,1,0:T(8,128)S(1)}, f32[3,88,128]{2,1,0:T(8,128)S(1)}, u32[]{:S(2)}, u32[]{:S(2)}) collective-permute-start(f32[3,88,128]{2,1,0:T(8,128)S(1)} %get-tuple-element.134.x_ref), channel_id=1, source_target_pairs={{1,2},{0,7},{3,4},{2,1},{5,6},{4,3},{7,0},{6,5},{9,10},{8,15},{11,... | collective-permute-start | bytes 405512 | tf_op jit(solution)/shard_map/ppermute | solution.py:410
  68.8 2.4 %collective-permute-start.10 = (f32[3,88,128]{2,1,0:T(8,128)S(1)}, f32[3,88,128]{2,1,0:T(8,128)S(1)}, u32[]{:S(2)}, u32[]{:S(2)}) collective-permute-start(f32[3,88,128]{2,1,0:T(8,128)S(1)} %collective-permute-done.9.o_ref), channel_id=1, source_target_pairs={{0,1},{1,0},{2,3},{3,2},{4,5},{5,4},{6,7},{7,6},{8,9},{9,8},{10,11... | collective-permute-start | bytes 405512 | tf_op jit(solution)/shard_map/ppermute | solution.py:419
  69.1 2.1 %collective-permute-start.11 = (f32[2,88,128]{2,1,0:T(8,128)S(1)}, f32[2,88,128]{2,1,0:T(8,128)S(1)}, u32[]{:S(2)}, u32[]{:S(2)}) collective-permute-start(f32[2,88,128]{2,1,0:T(8,128)S(1)} %get-tuple-element.146.rest_0_), channel_id=1, source_target_pairs={{0,1},{1,0},{2,3},{3,2},{4,5},{5,4},{6,7},{7,6},{8,9},{9,8},{10,11... | collective-permute-start | bytes 270344 | tf_op jit(solution)/shard_map/ppermute | solution.py:418
  73.9 5.0 %collective-permute-start.12 = (f32[3,88,128]{2,1,0:T(8,128)S(1)}, f32[3,88,128]{2,1,0:T(8,128)S(1)}, u32[]{:S(2)}, u32[]{:S(2)}) collective-permute-start(f32[3,88,128]{2,1,0:T(8,128)S(1)} %get-tuple-element.150.x_ref), channel_id=1, source_target_pairs={{1,2},{0,7},{3,4},{2,1},{5,6},{4,3},{7,0},{6,5},{9,10},{8,15},{11,... | collective-permute-start | bytes 405512 | tf_op jit(solution)/shard_map/ppermute | solution.py:410
  78.9 2.8 %collective-permute-start.13 = (f32[3,88,128]{2,1,0:T(8,128)S(1)}, f32[3,88,128]{2,1,0:T(8,128)S(1)}, u32[]{:S(2)}, u32[]{:S(2)}) collective-permute-start(f32[3,88,128]{2,1,0:T(8,128)S(1)} %collective-permute-done.12.o_ref), channel_id=1, source_target_pairs={{0,1},{1,0},{2,3},{3,2},{4,5},{5,4},{6,7},{7,6},{8,9},{9,8},{10,11... | collective-permute-start | bytes 405512 | tf_op jit(solution)/shard_map/ppermute | solution.py:419
  79.8 1.8 %collective-permute-start.14 = (f32[2,88,128]{2,1,0:T(8,128)S(1)}, f32[2,88,128]{2,1,0:T(8,128)S(1)}, u32[]{:S(2)}, u32[]{:S(2)}) collective-permute-start(f32[2,88,128]{2,1,0:T(8,128)S(1)} %get-tuple-element.162.rest_0_), channel_id=1, source_target_pairs={{0,1},{1,0},{2,3},{3,2},{4,5},{5,4},{6,7},{7,6},{8,9},{9,8},{10,11... | collective-permute-start | bytes 270344 | tf_op jit(solution)/shard_map/ppermute | solution.py:418
  84.3 5.1 %collective-permute-start.15 = (f32[3,88,128]{2,1,0:T(8,128)S(1)}, f32[3,88,128]{2,1,0:T(8,128)S(1)}, u32[]{:S(2)}, u32[]{:S(2)}) collective-permute-start(f32[3,88,128]{2,1,0:T(8,128)S(1)} %get-tuple-element.166.x_ref), channel_id=1, source_target_pairs={{1,2},{0,7},{3,4},{2,1},{5,6},{4,3},{7,0},{6,5},{9,10},{8,15},{11,... | collective-permute-start | bytes 405512 | tf_op jit(solution)/shard_map/ppermute | solution.py:410
  89.4 3.7 %collective-permute-start.16 = (f32[3,88,128]{2,1,0:T(8,128)S(1)}, f32[3,88,128]{2,1,0:T(8,128)S(1)}, u32[]{:S(2)}, u32[]{:S(2)}) collective-permute-start(f32[3,88,128]{2,1,0:T(8,128)S(1)} %collective-permute-done.15.o_ref), channel_id=1, source_target_pairs={{0,1},{1,0},{2,3},{3,2},{4,5},{5,4},{6,7},{7,6},{8,9},{9,8},{10,11... | collective-permute-start | bytes 405512 | tf_op jit(solution)/shard_map/ppermute | solution.py:419
  91.1 2.1 %collective-permute-start.17 = (f32[2,88,128]{2,1,0:T(8,128)S(1)}, f32[2,88,128]{2,1,0:T(8,128)S(1)}, u32[]{:S(2)}, u32[]{:S(2)}) collective-permute-start(f32[2,88,128]{2,1,0:T(8,128)S(1)} %get-tuple-element.178.rest_0_), channel_id=1, source_target_pairs={{0,1},{1,0},{2,3},{3,2},{4,5},{5,4},{6,7},{7,6},{8,9},{9,8},{10,11... | collective-permute-start | bytes 270344 | tf_op jit(solution)/shard_map/ppermute | solution.py:418
  95.9 4.8 %collective-permute-start.18 = (f32[3,88,128]{2,1,0:T(8,128)S(1)}, f32[3,88,128]{2,1,0:T(8,128)S(1)}, u32[]{:S(2)}, u32[]{:S(2)}) collective-permute-start(f32[3,88,128]{2,1,0:T(8,128)S(1)} %get-tuple-element.182.x_ref), channel_id=1, source_target_pairs={{1,2},{0,7},{3,4},{2,1},{5,6},{4,3},{7,0},{6,5},{9,10},{8,15},{11,... | collective-permute-start | bytes 405512 | tf_op jit(solution)/shard_map/ppermute | solution.py:410
  100.7 3.1 %collective-permute-start.19 = (f32[3,88,128]{2,1,0:T(8,128)S(1)}, f32[3,88,128]{2,1,0:T(8,128)S(1)}, u32[]{:S(2)}, u32[]{:S(2)}) collective-permute-start(f32[3,88,128]{2,1,0:T(8,128)S(1)} %collective-permute-done.18.o_ref), channel_id=1, source_target_pairs={{0,1},{1,0},{2,3},{3,2},{4,5},{5,4},{6,7},{7,6},{8,9},{9,8},{10,11... | collective-permute-start | bytes 405512 | tf_op jit(solution)/shard_map/ppermute | solution.py:419
  102.0 1.8 %collective-permute-start.20 = (f32[2,88,128]{2,1,0:T(8,128)S(1)}, f32[2,88,128]{2,1,0:T(8,128)S(1)}, u32[]{:S(2)}, u32[]{:S(2)}) collective-permute-start(f32[2,88,128]{2,1,0:T(8,128)S(1)} %get-tuple-element.194.rest_0_), channel_id=1, source_target_pairs={{0,1},{1,0},{2,3},{3,2},{4,5},{5,4},{6,7},{7,6},{8,9},{9,8},{10,11... | collective-permute-start | bytes 270344 | tf_op jit(solution)/shard_map/ppermute | solution.py:418
  106.9 4.7 %collective-permute-start.21 = (f32[3,88,128]{2,1,0:T(8,128)S(1)}, f32[3,88,128]{2,1,0:T(8,128)S(1)}, u32[]{:S(2)}, u32[]{:S(2)}) collective-permute-start(f32[3,88,128]{2,1,0:T(8,128)S(1)} %get-tuple-element.198.x_ref), channel_id=1, source_target_pairs={{1,2},{0,7},{3,4},{2,1},{5,6},{4,3},{7,0},{6,5},{9,10},{8,15},{11,... | collective-permute-start | bytes 405512 | tf_op jit(solution)/shard_map/ppermute | solution.py:432
  111.6 3.2 %collective-permute-start.22 = (f32[3,88,128]{2,1,0:T(8,128)S(1)}, f32[3,88,128]{2,1,0:T(8,128)S(1)}, u32[]{:S(2)}, u32[]{:S(2)}) collective-permute-start(f32[3,88,128]{2,1,0:T(8,128)S(1)} %collective-permute-done.21.o_ref), channel_id=1, source_target_pairs={{0,1},{1,0},{2,3},{3,2},{4,5},{5,4},{6,7},{7,6},{8,9},{9,8},{10,11... | collective-permute-start | bytes 405512 | tf_op jit(solution)/shard_map/ppermute | solution.py:435
